TPU v7x, 32 devices: a whole 2x2x4 slice. The times are simulated.
32 devices in a mesh: segment: 4 (over z), ctx: 2 (over x), dp: 4 (over y, core).
Axes of the slice: x: 2, y: 2, z: 4, core: 2. Of those that a mesh axis runs over, the one named last changes fastest.
Arguments:
- qkv: bfloat16 [4, 4, 320, 3, 2560], P('segment', 'dp', 'ctx'), may hold values from -24 to 24
- qk_gain: float32 [4, 2, 2560], P('segment'), may hold values from 1.5 to 2.5
- mod_weight: float32 [4, 256, 2560], P('segment'), may hold values from -0.375 to 0.375
- positions: int32 [4, 320], P('dp', 'ctx'), may hold values from 0 to 75599
- timesteps: int32 [4, 4], P('segment', 'dp'), may hold values from 0 to 999
- cotangent: bfloat16 [4, 4, 320, 2560], P('segment', 'dp', 'ctx'), may hold values from -6 to 6
Outputs:
- attn_out: bfloat16 [4, 4, 320, 2560], P('segment', 'dp', 'ctx')
- gate_grad: float32 [4, 256, 2560], P('segment', ('ctx', 'dp'))
All inputs are finite; a program needn't handle non-finite values.
Results may differ from a plain program's by a relative error of at most 0.012.
Values may be sent and summed in bfloat16 or wider, within the bound.
A program may use at most 128 MiB of HBM per device.

v0:
```python
import functools
import math

import jax
import jax.numpy as jnp
from jax import lax
from jax.experimental import pallas as pl
from jax.experimental.pallas import tpu as pltpu
from jax.sharding import PartitionSpec as P

HEAD_DIM = 128
GRID_ROWS = 45
GRID_COLS = 80
MESH = pl.DeviceIdType.MESH
LEAD = 8
LAG = 6
DIRECT = 5
FORWARD_AT = 6
VMEM_LIMIT = 24 << 20


def sincos(angle):
    turns = jnp.floor(angle * (2.0 / math.pi) + 0.5)
    quad = turns.astype(jnp.int32)
    r = angle - turns * 1.5703125
    r = r - turns * 4.837512969970703125e-4
    r = r - turns * 7.549789948768648e-8
    z = r * r
    sine = r + r * z * (-1.6666654611e-1 + z * (8.3321608736e-3 - z * 1.9515295891e-4))
    cosine = 1.0 - 0.5 * z + z * z * (
        4.166664568298827e-2 + z * (-1.388731625493765e-3 + z * 2.443315711809948e-5)
    )
    swap = (quad & 1) == 1
    s = jnp.where(swap, cosine, sine)
    c = jnp.where(swap, sine, cosine)
    s = jnp.where((quad & 2) == 2, -s, s)
    c = jnp.where(((quad + 1) & 2) == 2, -c, c)
    return s, c


def rope_angles(pos):
    count, hd = pos.shape
    half = hd // 2
    side = hd // 6
    first = half - 2 * side
    pair = lax.broadcasted_iota(jnp.int32, (8, hd), 1) % half
    group = jnp.where(pair < first, 0, jnp.where(pair < first + side, 1, 2))
    offset = jnp.where(group == 0, 0, jnp.where(group == 1, first, first + side))
    pairs_in = jnp.where(group == 0, first, side).astype(jnp.float32)
    freq = jnp.exp((pair - offset).astype(jnp.float32) / pairs_in * -math.log(10000.0))[0:1]
    group = group[0:1]
    frame = (pos // (GRID_ROWS * GRID_COLS)).astype(jnp.float32)
    row = (pos // GRID_COLS % GRID_ROWS).astype(jnp.float32)
    col = (pos % GRID_COLS).astype(jnp.float32)
    return jnp.where(group == 0, frame, jnp.where(group == 1, row, col)) * freq


def body(
    S, C, D, heads, freqs,
    x_ref, gain_ref, w_ref, pos_ref, t_ref, cot_ref,
    out_ref, cbuf, ebuf,
    xv, wv, cotv, kv, qbuf, abuf, rbuf, direct, gains, tbuf, gate, cosv, sinv,
    load_sem, kv_send, kv_recv, a_send, a_recv, g_send, g_recv, t_send, t_recv, c_send, c_recv,
    b_send, b_recv, bx_send, bx_recv, down_sem, up_sem,
):
    n = C * D
    count = x_ref.shape[1]
    rows = freqs // n
    hd = HEAD_DIM
    early = heads - direct.shape[0]
    seg = lax.axis_index("segment")
    ctx = lax.axis_index("ctx")
    dp = lax.axis_index("dp")
    me = ctx * D + dp
    after = {"segment": lax.rem(seg + 1, S)}
    before = {"segment": lax.rem(seg + S - 1, S)}
    peers = []
    for r in range(1, n):
        p = lax.rem(me + r, n)
        peers.append({"ctx": p // D, "dp": lax.rem(p, D)})
    ring = [{"ctx": lax.rem(ctx + r, C)} for r in range(1, C)]

    def cols(h):
        return pl.ds(pl.multiple_of(h * hd, hd), hd)

    loads = [
        pltpu.make_async_copy(x_ref.at[1], xv.at[1], load_sem.at[1]),
        pltpu.make_async_copy(x_ref.at[0], xv.at[0], load_sem.at[0]),
        pltpu.make_async_copy(x_ref.at[2], xv.at[2], load_sem.at[2]),
        pltpu.make_async_copy(w_ref, wv, load_sem.at[3]),
        pltpu.make_async_copy(cot_ref, cotv, load_sem.at[4]),
    ]
    for load in loads:
        load.start()
    step = t_ref[0, 0].astype(jnp.float32)
    tbuf[0] = jnp.full((8, hd), step, jnp.float32)

    barrier = pltpu.get_barrier_semaphore()
    def greet(who):
        pl.semaphore_signal(barrier, inc=1, device_id=who, device_id_type=MESH)

    for who in peers:
        greet(who)
    chain = S > 2
    if chain:
        @pl.when(seg < S - 1)
        def _():
            greet(after)

        @pl.when(seg > 0)
        def _():
            greet(before)

        ends = jnp.where(seg == 0, 1, 0) + jnp.where(seg == S - 1, 1, 0)
        pl.semaphore_wait(barrier, n + 1 - ends)
    else:
        greet(after)
        greet(before)
        pl.semaphore_wait(barrier, n + 1)

    gain_copy = pltpu.make_async_remote_copy(
        src_ref=gain_ref, dst_ref=gains, send_sem=g_send, recv_sem=g_recv,
        device_id=before, device_id_type=MESH,
    )

    def send_values(h):
        for r in range(1, C):
            pltpu.make_async_remote_copy(
                src_ref=x_ref.at[2, :, cols(h)],
                dst_ref=kv.at[h, 1, pl.ds(r * count, count), :],
                send_sem=kv_send.at[h], recv_sem=kv_recv.at[h],
                device_id=ring[r - 1], device_id_type=MESH,
            ).start()

    def send_keys(h):
        for r in range(1, C):
            pltpu.make_async_remote_copy(
                src_ref=kv.at[h, 0, pl.ds(0, count), :],
                dst_ref=kv.at[h, 0, pl.ds(r * count, count), :],
                send_sem=kv_send.at[h], recv_sem=kv_recv.at[h],
                device_id=ring[r - 1], device_id_type=MESH,
            ).start()

    lead = min(LEAD, early)

    @pl.loop(0, lead)
    def _(h):
        send_values(h)

    for r in range(1, n):
        pltpu.make_async_remote_copy(
            src_ref=tbuf.at[0], dst_ref=tbuf.at[r], send_sem=t_send, recv_sem=t_recv,
            device_id=peers[r - 1], device_id_type=MESH,
        ).start()

    def tell(sem, who):
        pl.semaphore_signal(sem, inc=1, device_id=who, device_id_type=MESH)

    if chain:
        @pl.when(seg > 0)
        def _():
            gain_copy.start()

        @pl.when(seg == S - 2)
        def _():
            tell(down_sem, before)

        @pl.when(seg == 1)
        def _():
            tell(up_sem, after)

        @pl.when(seg < S - 2)
        def _():
            pl.semaphore_wait(down_sem, 1)

            @pl.when(seg > 0)
            def _():
                tell(down_sem, before)

        @pl.when(seg == 0)
        def _():
            gain_copy.start()

        @pl.when(seg > 1)
        def _():
            pl.semaphore_wait(up_sem, 1)

            @pl.when(seg < S - 1)
            def _():
                tell(up_sem, after)
    else:
        gain_copy.start()

    pos = jnp.transpose(jnp.broadcast_to(pos_ref[...], (hd, count)))
    s, c = sincos(rope_angles(pos))
    lane = lax.broadcasted_iota(jnp.int32, (count, hd), 1)
    cosv[...] = c
    sinv[...] = jnp.where(lane < hd // 2, -s, s)

    def inverse_norm(which):
        def add(h, acc):
            x = xv[which, :, cols(h)].astype(jnp.float32)
            return acc + x * x

        total = lax.fori_loop(0, heads, add, jnp.zeros((count, hd), jnp.float32))
        mean = jnp.sum(total, axis=1, keepdims=True) / (heads * hd)
        return lax.rsqrt(mean + 1e-06)

    def turned(which, h, inv):
        x = xv[which, :, cols(h)].astype(jnp.float32)
        x = x * inv * gains[which : which + 1, cols(h)]
        return (x * cosv[...] + pltpu.roll(x, hd // 2, 1) * sinv[...]).astype(jnp.bfloat16)

    loads[0].wait()
    inv_k = inverse_norm(1)
    loads[1].wait()
    inv_q = inverse_norm(0)
    gain_copy.wait_recv()

    def hand_over(source, part, b):
        pltpu.make_async_remote_copy(
            src_ref=source, dst_ref=direct.at[b, part, pl.ds(0, count), :],
            send_sem=b_send.at[b], recv_sem=b_recv.at[b], device_id=after, device_id_type=MESH,
        ).start()

    def forward(b):
        here = direct.at[b, :, pl.ds(0, count), :]
        pltpu.make_async_copy(here, here, b_recv.at[b]).wait()
        for r in range(1, C):
            pltpu.make_async_remote_copy(
                src_ref=direct.at[b, pl.ds(0, 2), pl.ds(0, count), :],
                dst_ref=direct.at[b, pl.ds(0, 2), pl.ds(r * count, count), :],
                send_sem=bx_send.at[b], recv_sem=bx_recv.at[b],
                device_id=ring[r - 1], device_id_type=MESH,
            ).start()

    @pl.loop(early, heads)
    def _(h):
        kv[h, 0, 0:count, :] = turned(1, h, inv_k)
        qbuf[h] = turned(0, h, inv_q)
        hand_over(x_ref.at[2, :, cols(h)], 1, h - early)
        hand_over(kv.at[h, 0, pl.ds(0, count), :], 0, h - early)
        hand_over(qbuf.at[h], 2, h - early)

    @pl.loop(0, early)
    def _(h):
        kv[h, 0, 0:count, :] = turned(1, h, inv_k)
        send_keys(h)

        @pl.when(h + lead < early)
        def _():
            send_values(h + lead)

    loads[2].wait()

    @pl.loop(0, early)
    def _(h):
        qbuf[h] = turned(0, h, inv_q)
        kv[h, 1, 0:count, :] = xv[2, :, cols(h)]

    half = freqs // 2
    decay = -math.log(10000.0) / half
    index = lax.broadcasted_iota(jnp.int32, (half, hd), 0).astype(jnp.float32)
    es, ec = sincos(step * jnp.exp(index * decay))
    loads[3].wait()

    @pl.loop(0, heads)
    def _(h):
        part = wv[0:half, cols(h)] * ec + wv[half:freqs, cols(h)] * es
        gate[pl.ds(h, 1), :] = jnp.sum(part, axis=0, keepdims=True)

    if n > 1:
        pltpu.make_async_copy(tbuf.at[pl.ds(1, n - 1)], tbuf.at[pl.ds(1, n - 1)], t_recv).wait()
    at = lax.broadcasted_iota(jnp.int32, (rows, hd), 0) + me * rows
    freq = jnp.exp((at % half).astype(jnp.float32) * decay)
    for j in range(n):
        s, c = sincos(tbuf[j, 0:1, :] * freq)
        ebuf[j] = jnp.where(at < half, c, s)
    loads[4].wait()

    scale = 1.0 / hd**0.5

    def mix(queries, keys, values):
        scores = lax.dot_general(
            queries, keys, (((1,), (1,)), ((), ())), preferred_element_type=jnp.float32
        ) * scale
        expo = jnp.exp(scores - jnp.max(scores, axis=1, keepdims=True))
        total = jnp.sum(expo, axis=1, keepdims=True)
        mixed = jnp.dot(expo.astype(jnp.bfloat16), values, preferred_element_type=jnp.float32)
        return mixed / total

    def attend(h):
        arrived = kv.at[h, :, pl.ds(count, (C - 1) * count), :]
        pltpu.make_async_copy(arrived, arrived, kv_recv.at[h]).wait()
        abuf[h] = mix(qbuf[h], kv[h, 0], kv[h, 1]).astype(jnp.bfloat16)
        pltpu.make_async_remote_copy(
            src_ref=abuf.at[h], dst_ref=rbuf.at[h], send_sem=a_send.at[h], recv_sem=a_recv.at[h],
            device_id=after, device_id_type=MESH,
        ).start()

    def use(h, attn):
        out_ref[:, cols(h)] = (attn * gate[pl.ds(h, 1), :]).astype(jnp.bfloat16)
        cot = cotv[:, cols(h)].astype(jnp.float32)
        cbuf[0, pl.ds(h, 1), :] = jnp.sum(attn * cot, axis=0, keepdims=True)

    def finish(h):
        pltpu.make_async_copy(rbuf.at[h], rbuf.at[h], a_recv.at[h]).wait()
        use(h, rbuf[h].astype(jnp.float32))

    @pl.loop(0, early)
    def _(h):
        attend(h)

        @pl.when(h == min(FORWARD_AT, early - 1))
        def _():
            @pl.loop(0, heads - early)
            def _(b):
                forward(b)

        @pl.when(h >= LAG)
        def _():
            finish(h - LAG)

    @pl.loop(max(early - LAG, 0), early)
    def _(h):
        finish(h)

    split = early // 8 * 8

    def share_sums(low, high, part):
        for r in range(1, n):
            pltpu.make_async_remote_copy(
                src_ref=cbuf.at[0, pl.ds(low, high - low), :],
                dst_ref=cbuf.at[r, pl.ds(low, high - low), :],
                send_sem=c_send.at[part], recv_sem=c_recv.at[part],
                device_id=peers[r - 1], device_id_type=MESH,
            ).start()

    if split > 0:
        share_sums(0, split, 0)

    @pl.loop(early, heads)
    def _(h):
        b = h - early
        arrived = direct.at[b, pl.ds(0, 2), pl.ds(count, (C - 1) * count), :]
        pltpu.make_async_copy(arrived, arrived, bx_recv.at[b]).wait()
        use(h, mix(direct[b, 2, 0:count, :], direct[b, 0], direct[b, 1]))

    if n > 1:
        share_sums(split, cbuf.shape[1], 1)
        for part, (low, high) in enumerate(((0, split), (split, cbuf.shape[1]))):
            if high > low:
                others = cbuf.at[pl.ds(1, n - 1), pl.ds(low, high - low), :]
                pltpu.make_async_copy(others, others, c_recv.at[part]).wait()

    gain_copy.wait_send()
    pltpu.make_async_copy(tbuf.at[pl.ds(1, n - 1)], tbuf.at[pl.ds(1, n - 1)], t_send).wait()
    for part, (low, high) in enumerate(((0, split), (split, cbuf.shape[1]))):
        if n > 1 and high > low:
            others = cbuf.at[pl.ds(1, n - 1), pl.ds(low, high - low), :]
            pltpu.make_async_copy(others, others, c_send.at[part]).wait()

    @pl.loop(0, heads - early)
    def _(b):
        handed = direct.at[b, :, pl.ds(0, count), :]
        pltpu.make_async_copy(handed, handed, b_send.at[b]).wait()
        sent = direct.at[b, pl.ds(0, 2), pl.ds(count, (C - 1) * count), :]
        pltpu.make_async_copy(sent, sent, bx_send.at[b]).wait()

    @pl.loop(0, early)
    def _(h):
        sent = kv.at[h, :, pl.ds(count, (C - 1) * count), :]
        pltpu.make_async_copy(sent, sent, kv_send.at[h]).wait()
        pltpu.make_async_copy(abuf.at[h], abuf.at[h], a_send.at[h]).wait()


def store(n, heads, attn_ref, chan_ref, emb_ref, out_ref, grad_ref, total, out_sem, grad_sem):
    copy = pltpu.make_async_copy(attn_ref, out_ref, out_sem)
    copy.start()
    hd = HEAD_DIM
    for h in range(heads):
        acc = emb_ref[0] * chan_ref[0, h : h + 1, :]
        for j in range(1, n):
            acc = acc + emb_ref[j] * chan_ref[j, h : h + 1, :]
        total[h] = acc
        pltpu.make_async_copy(total.at[h], grad_ref.at[:, h * hd : (h + 1) * hd], grad_sem.at[h]).start()
    for h in range(heads):
        pltpu.make_async_copy(total.at[h], grad_ref.at[:, h * hd : (h + 1) * hd], grad_sem.at[h]).wait()
    copy.wait()


def local(S, C, D, qkv, qk_gain, mod_weight, positions, timesteps, cotangent):
    count, _, width = qkv.shape[2:]
    freqs = mod_weight.shape[1]
    heads = width // HEAD_DIM
    n = C * D
    rows = freqs // n
    hd = HEAD_DIM
    last = min(DIRECT, heads - 1)
    padded = -(-heads // 8) * 8
    bf, f32 = jnp.bfloat16, jnp.float32
    vmem = pl.BlockSpec(memory_space=pltpu.VMEM)
    hbm = pl.BlockSpec(memory_space=pltpu.HBM)
    dma = pltpu.SemaphoreType.DMA
    pin = functools.partial(pltpu.with_memory_space_constraint, memory_space=pltpu.HBM)
    attn, chans, embs = pl.pallas_call(
        functools.partial(body, S, C, D, heads, freqs),
        out_shape=(
            jax.ShapeDtypeStruct((count, width), bf),
            jax.ShapeDtypeStruct((n, padded, hd), f32),
            jax.ShapeDtypeStruct((n, rows, hd), f32),
        ),
        in_specs=[hbm, hbm, hbm, vmem, pl.BlockSpec(memory_space=pltpu.SMEM), hbm],
        out_specs=(vmem, vmem, vmem),
        scratch_shapes=[
            pltpu.VMEM((3, count, width), bf),
            pltpu.VMEM((freqs, width), f32),
            pltpu.VMEM((count, width), bf),
            pltpu.VMEM((heads, 2, C * count, hd), bf),
            pltpu.VMEM((heads, count, hd), bf),
            pltpu.VMEM((heads, count, hd), bf),
            pltpu.VMEM((heads, count, hd), bf),
            pltpu.VMEM((last, 3, C * count, hd), bf),
            pltpu.VMEM((2, width), f32),
            pltpu.VMEM((n, 8, hd), f32),
            pltpu.VMEM((padded, hd), f32),
            pltpu.VMEM((count, hd), f32),
            pltpu.VMEM((count, hd), f32),
            dma((5,)),
            dma((heads,)), dma((heads,)), dma((heads,)), dma((heads,)),
            dma, dma, dma, dma, dma((2,)), dma((2,)),
            dma((last,)), dma((last,)), dma((last,)), dma((last,)),
            pltpu.SemaphoreType.REGULAR, pltpu.SemaphoreType.REGULAR,
        ],
        compiler_params=pltpu.CompilerParams(
            collective_id=0, has_side_effects=True, vmem_limit_bytes=VMEM_LIMIT if C <= 2 else 60 << 20
        ),
    )(
        pin(jnp.moveaxis(qkv[0, 0], 1, 0)),
        pin(qk_gain[0]),
        pin(mod_weight[0]),
        pin(positions),
        timesteps,
        pin(cotangent[0, 0]),
    )
    attn_out, grad = pl.pallas_call(
        functools.partial(store, n, heads),
        out_shape=(
            jax.ShapeDtypeStruct((count, width), bf),
            jax.ShapeDtypeStruct((rows, width), f32),
        ),
        in_specs=[pl.BlockSpec(memory_space=pl.ANY), vmem, vmem],
        out_specs=(pl.BlockSpec(memory_space=pl.ANY), pl.BlockSpec(memory_space=pl.ANY)),
        scratch_shapes=[pltpu.VMEM((heads, rows, hd), f32), dma, dma((heads,))],
        compiler_params=pltpu.CompilerParams(vmem_limit_bytes=4 << 20),
    )(attn, chans, embs)
    return attn_out[None, None], grad[None]


def solution(mesh):
    sizes = mesh.shape
    return jax.shard_map(
        functools.partial(local, sizes["segment"], sizes["ctx"], sizes["dp"]),
        mesh=mesh,
        in_specs=(
            P("segment", "dp", "ctx", None, None),
            P("segment", None, None),
            P("segment", None, None),
            P("dp", "ctx"),
            P("segment", "dp"),
            P("segment", "dp", "ctx", None),
        ),
        out_specs=(P("segment", "dp", "ctx", None), P("segment", ("ctx", "dp"), None)),
        check_vma=False,
    )
```

profile of v0, /device:TPU:0, one launch (start us, length us, event | category | flops | bytes accessed | tf_op | source)
XLA Modules:
  0.0 49.2 jit_solution(15449150682975746735)
XLA Ops:
  1.3 46.7 %shard_map.77 = (bf16[160,2560]{1,0:T(8,128)(2,1)S(1)}, f32[8,24,128]{2,1,0:T(8,128)S(1)}, f32[8,32,128]{2,1,0:T(8,128)S(1)}) custom-call(bf16[3,160,2560]{2,1,0:T(8,128)(2,1)} %bitcast.9, f32[2,2560]{1,0:T(2,128)} %bitcast.11, f32[256,2560]{1,0:T(8,128)} %bitcast.8, s32[1,160]{1,0:T(1,128)} %pos_ref.1, s32[1,1]{1,0:T(1,128)S(6)} %copy.8.t_ref, ...), custom_call_target="tpu_custom_call" | custom-call | tf_op jit(solution)/shard_map/pallas_call | solution.py:406
  48.0 1.2 %shard_map.78 = (bf16[160,2560]{1,0:T(8,128)(2,1)}, f32[32,2560]{1,0:T(8,128)}) custom-call(bf16[160,2560]{1,0:T(8,128)(2,1)S(1)} %get-tuple-element.7.attn_ref, f32[8,24,128]{2,1,0:T(8,128)S(1)} %get-tuple-element.8.chan_ref, f32[8,32,128]{2,1,0:T(8,128)S(1)} %get-tuple-element.9.emb_ref), custom_call_target="tpu_custom_call" | custom-call | tf_op jit(solution)/shard_map/pallas_call | solution.py:446
where the time goes:
time: 49.3 us; the launch traced here: 49.2 us
  Pallas kernels  47.9 us (97%)
  between operations  1.29 us (3%)
    pallas_call x1, Pallas kernels, local(): pl.pallas_call(functools.partial(body, S, C, D, heads, freqs), out_shape=...  46.7 us
    pallas_call x1, Pallas kernels, local(): pl.pallas_call(functools.partial(store, n, heads), out_shape=(jax.ShapeDt...  1.17 us

commit v1 on v0

v1 whole, which is shorter than its diff:
```python
import functools
import math

import jax
import jax.numpy as jnp
from jax import lax
from jax.experimental import pallas as pl
from jax.experimental.pallas import tpu as pltpu
from jax.sharding import PartitionSpec as P

HEAD_DIM = 128
GRID_ROWS = 45
GRID_COLS = 80
MESH = pl.DeviceIdType.MESH
LEAD = 12
LAG = 6
DIRECT = 5
BONUS = 0
TAIL = 8
FORWARD_AT = 8
VMEM_LIMIT = 24 << 20


def sincos(angle):
    turns = jnp.floor(angle * (2.0 / math.pi) + 0.5)
    quad = turns.astype(jnp.int32)
    r = angle - turns * 1.5703125
    r = r - turns * 4.837512969970703125e-4
    r = r - turns * 7.549789948768648e-8
    z = r * r
    sine = r + r * z * (-1.6666654611e-1 + z * (8.3321608736e-3 - z * 1.9515295891e-4))
    cosine = 1.0 - 0.5 * z + z * z * (
        4.166664568298827e-2 + z * (-1.388731625493765e-3 + z * 2.443315711809948e-5)
    )
    swap = (quad & 1) == 1
    s = jnp.where(swap, cosine, sine)
    c = jnp.where(swap, sine, cosine)
    s = jnp.where((quad & 2) == 2, -s, s)
    c = jnp.where(((quad + 1) & 2) == 2, -c, c)
    return s, c


def rope_angles(pos):
    count, hd = pos.shape
    half = hd // 2
    side = hd // 6
    first = half - 2 * side
    pair = lax.broadcasted_iota(jnp.int32, (8, hd), 1) % half
    group = jnp.where(pair < first, 0, jnp.where(pair < first + side, 1, 2))
    offset = jnp.where(group == 0, 0, jnp.where(group == 1, first, first + side))
    pairs_in = jnp.where(group == 0, first, side).astype(jnp.float32)
    freq = jnp.exp((pair - offset).astype(jnp.float32) / pairs_in * -math.log(10000.0))[0:1]
    group = group[0:1]
    frame = (pos // (GRID_ROWS * GRID_COLS)).astype(jnp.float32)
    row = (pos // GRID_COLS % GRID_ROWS).astype(jnp.float32)
    col = (pos % GRID_COLS).astype(jnp.float32)
    return jnp.where(group == 0, frame, jnp.where(group == 1, row, col)) * freq


def handed(seg, S):
    return DIRECT + jnp.where(seg == 0, BONUS, 0)


def body(
    S, C, D, heads, freqs,
    x_ref, gain_ref, w_ref, pos_ref, t_ref, cot_ref,
    out_ref, grad_ref,
    xv, wv, cotv, kv, qbuf, abuf, rbuf, direct, gains, posv, tbuf, gate, emb, cosv, sinv,
    part, total, late,
    load_sem, v_sem, kv_send, kv_recv, a_send, a_recv, g_send, g_recv, t_send, t_recv,
    p_send, p_recv, c_send, c_recv, l_send, l_recv,
    b_send, b_recv, bx_send, bx_recv, in_sem, down_sem, up_sem, met_sem,
):
    n = C * D
    count = x_ref.shape[1]
    rows = freqs // n
    hd = HEAD_DIM
    tail = late.shape[1]
    first = heads - tail
    seg = lax.axis_index("segment")
    ctx = lax.axis_index("ctx")
    dp = lax.axis_index("dp")
    me = ctx * D + dp
    after = {"segment": lax.rem(seg + 1, S)}
    before = {"segment": lax.rem(seg + S - 1, S)}
    early = heads - handed(seg, S)
    landed = heads - handed(before["segment"], S)
    peers = []
    for r in range(1, n):
        p = lax.rem(me + r, n)
        peers.append({"ctx": p // D, "dp": lax.rem(p, D)})
    ring = [{"ctx": lax.rem(ctx + r, C)} for r in range(1, C)]
    clips = [{"dp": lax.rem(dp + r, D)} for r in range(1, D)]

    def cols(h):
        return pl.ds(pl.multiple_of(h * hd, hd), hd)

    def tell(sem, who):
        pl.semaphore_signal(sem, inc=1, device_id=who, device_id_type=MESH)

    barrier = pltpu.get_barrier_semaphore()
    for who in ring + clips:
        tell(barrier, who)

    @pl.when(seg < S - 1)
    def _():
        tell(barrier, after)

    loads = [
        pltpu.make_async_copy(pos_ref, posv, load_sem.at[0]),
        pltpu.make_async_copy(x_ref.at[1], xv.at[1], load_sem.at[1]),
        pltpu.make_async_copy(x_ref.at[0], xv.at[0], load_sem.at[2]),
        pltpu.make_async_copy(w_ref, wv, load_sem.at[3]),
        pltpu.make_async_copy(cot_ref, cotv, load_sem.at[4]),
    ]
    for load in loads:
        load.start()

    pl.semaphore_wait(barrier, C - 1 + D - 1 + jnp.where(seg > 0, 1, 0))

    def send_values(h):
        for r in range(1, C):
            pltpu.make_async_remote_copy(
                src_ref=x_ref.at[2, :, cols(h)],
                dst_ref=kv.at[h, 1, pl.ds(r * count, count), :],
                send_sem=kv_send.at[h], recv_sem=kv_recv.at[h],
                device_id=ring[r - 1], device_id_type=MESH,
            ).start()

    def send_keys(h):
        for r in range(1, C):
            pltpu.make_async_remote_copy(
                src_ref=kv.at[h, 0, pl.ds(0, count), :],
                dst_ref=kv.at[h, 0, pl.ds(r * count, count), :],
                send_sem=kv_send.at[h], recv_sem=kv_recv.at[h],
                device_id=ring[r - 1], device_id_type=MESH,
            ).start()

    lead = min(LEAD, heads - DIRECT - BONUS)

    @pl.loop(0, lead)
    def _(h):
        send_values(h)

    for who in ring:
        tell(met_sem, who)

    gain_copy = pltpu.make_async_remote_copy(
        src_ref=gain_ref, dst_ref=gains, send_sem=g_send, recv_sem=g_recv,
        device_id=before, device_id_type=MESH,
    )

    @pl.when(seg > 0)
    def _():
        tell(in_sem, before)
        gain_copy.start()

    @pl.when(seg < S - 1)
    def _():
        pl.semaphore_wait(in_sem, 1)

    @pl.when(seg == S - 2)
    def _():
        tell(down_sem, before)

    @pl.when(seg == 1)
    def _():
        tell(up_sem, after)

    @pl.when(seg < S - 2)
    def _():
        pl.semaphore_wait(down_sem, 1)

        @pl.when(seg > 0)
        def _():
            tell(down_sem, before)

    @pl.when(seg == 0)
    def _():
        gain_copy.start()

    @pl.when(seg > 1)
    def _():
        pl.semaphore_wait(up_sem, 1)

        @pl.when(seg < S - 1)
        def _():
            tell(up_sem, after)

    def hand_over(source, which, h):
        slot = heads - 1 - h
        pltpu.make_async_remote_copy(
            src_ref=source, dst_ref=direct.at[slot, which, pl.ds(0, count), :],
            send_sem=b_send.at[slot], recv_sem=b_recv.at[slot], device_id=after, device_id_type=MESH,
        ).start()

    def own_values(h):
        return pltpu.make_async_copy(
            x_ref.at[2, :, cols(h)], kv.at[h, 1, pl.ds(0, count), :], v_sem.at[h]
        )

    @pl.loop(early, heads)
    def _(h):
        hand_over(x_ref.at[2, :, cols(h)], 1, h)

    @pl.loop(0, early)
    def _(h):
        own_values(h).start()

    loads[0].wait()
    pos = jnp.transpose(jnp.broadcast_to(posv[...], (hd, count)))
    s, c = sincos(rope_angles(pos))
    lane = lax.broadcasted_iota(jnp.int32, (count, hd), 1)
    cosv[...] = c
    sinv[...] = jnp.where(lane < hd // 2, -s, s)

    tbuf[0] = jnp.full((8, hd), t_ref[0, 0].astype(jnp.float32), jnp.float32)
    for r in range(1, D):
        pltpu.make_async_remote_copy(
            src_ref=tbuf.at[0], dst_ref=tbuf.at[r], send_sem=t_send, recv_sem=t_recv,
            device_id=clips[r - 1], device_id_type=MESH,
        ).start()

    def inverse_norm(which):
        def add(h, acc):
            x = xv[which, :, cols(h)].astype(jnp.float32)
            return acc + x * x

        acc = lax.fori_loop(0, heads, add, jnp.zeros((count, hd), jnp.float32))
        mean = jnp.sum(acc, axis=1, keepdims=True) / (heads * hd)
        return lax.rsqrt(mean + 1e-06)

    def turned(which, h, inv):
        x = xv[which, :, cols(h)].astype(jnp.float32)
        x = x * inv * gains[which : which + 1, cols(h)]
        return (x * cosv[...] + pltpu.roll(x, hd // 2, 1) * sinv[...]).astype(jnp.bfloat16)

    loads[1].wait()
    inv_k = inverse_norm(1)
    loads[2].wait()
    inv_q = inverse_norm(0)
    gain_copy.wait_recv()

    def forward(slot):
        here = direct.at[slot, :, pl.ds(0, count), :]
        pltpu.make_async_copy(here, here, b_recv.at[slot]).wait()
        for which in range(2):
            for r in range(1, C):
                pltpu.make_async_remote_copy(
                    src_ref=direct.at[slot, which, pl.ds(0, count), :],
                    dst_ref=direct.at[slot, which, pl.ds(r * count, count), :],
                    send_sem=bx_send.at[slot, which], recv_sem=bx_recv.at[slot, which],
                    device_id=ring[r - 1], device_id_type=MESH,
                ).start()

    @pl.loop(early, heads)
    def _(h):
        kv[h, 0, 0:count, :] = turned(1, h, inv_k)
        qbuf[h] = turned(0, h, inv_q)
        hand_over(kv.at[h, 0, pl.ds(0, count), :], 0, h)
        hand_over(qbuf.at[h], 2, h)

    @pl.loop(0, early)
    def _(h):
        kv[h, 0, 0:count, :] = turned(1, h, inv_k)
        send_keys(h)

        @pl.when(h + lead < early)
        def _():
            send_values(h + lead)

    @pl.loop(0, early)
    def _(h):
        qbuf[h] = turned(0, h, inv_q)

    half = freqs // 2
    decay = -math.log(10000.0) / half
    index = lax.broadcasted_iota(jnp.int32, (half, hd), 0).astype(jnp.float32)
    es, ec = sincos(tbuf[0, 0:1, :] * jnp.exp(index * decay))
    loads[3].wait()

    @pl.loop(0, heads)
    def _(h):
        terms = wv[0:half, cols(h)] * ec + wv[half:freqs, cols(h)] * es
        gate[pl.ds(h, 1), :] = jnp.sum(terms, axis=0, keepdims=True)

    if D > 1:
        others = tbuf.at[pl.ds(1, D - 1)]
        pltpu.make_async_copy(others, others, t_recv).wait()
    at = lax.broadcasted_iota(jnp.int32, (rows, hd), 0) + me * rows
    freq = jnp.exp((at % half).astype(jnp.float32) * decay)
    for j in range(D):
        s, c = sincos(tbuf[j, 0:1, :] * freq)
        emb[j] = jnp.where(at < half, c, s)
    loads[4].wait()

    scale = 1.0 / hd**0.5

    def weigh(queries, keys):
        scores = lax.dot_general(
            queries, keys, (((1,), (1,)), ((), ())), preferred_element_type=jnp.float32
        ) * scale
        expo = jnp.exp(scores - jnp.max(scores, axis=1, keepdims=True))
        return expo.astype(jnp.bfloat16), jnp.sum(expo, axis=1, keepdims=True)

    def attend(h):
        own_values(h).wait()
        arrived = kv.at[h, :, pl.ds(count, (C - 1) * count), :]
        pltpu.make_async_copy(arrived, arrived, kv_recv.at[h]).wait()
        weights, norm = weigh(qbuf[h], kv[h, 0])
        mixed = jnp.dot(weights, kv[h, 1], preferred_element_type=jnp.float32)
        abuf[h] = (mixed / norm).astype(jnp.bfloat16)
        pltpu.make_async_remote_copy(
            src_ref=abuf.at[h], dst_ref=rbuf.at[h], send_sem=a_send.at[h], recv_sem=a_recv.at[h],
            device_id=after, device_id_type=MESH,
        ).start()

    def use(h, attn):
        out_ref[:, cols(h)] = (attn * gate[pl.ds(h, 1), :]).astype(jnp.bfloat16)
        cot = cotv[:, cols(h)].astype(jnp.float32)
        return jnp.sum(attn * cot, axis=0, keepdims=True)

    def finish(h):
        pltpu.make_async_copy(rbuf.at[h], rbuf.at[h], a_recv.at[h]).wait()
        return use(h, rbuf[h].astype(jnp.float32))

    @pl.loop(0, early)
    def _(h):
        attend(h)

        @pl.when(h == FORWARD_AT)
        def _():
            @pl.loop(landed, heads - 1)
            def _(g):
                forward(heads - 1 - g)

        @pl.when(h >= LAG)
        def _():
            part[0, pl.ds(h - LAG, 1), :] = finish(h - LAG)

    @pl.loop(early - LAG, first)
    def _(h):
        part[0, pl.ds(h, 1), :] = finish(h)

    for r in range(1, C):
        pltpu.make_async_remote_copy(
            src_ref=part.at[0], dst_ref=part.at[r], send_sem=p_send, recv_sem=p_recv,
            device_id=ring[r - 1], device_id_type=MESH,
        ).start()
    forward(0)

    @pl.loop(first, landed)
    def _(h):
        late[0, pl.ds(h - first, 1), :] = finish(h)

    def direct_head(h):
        slot = heads - 1 - h
        arrived = direct.at[slot, 0, pl.ds(count, (C - 1) * count), :]
        pltpu.make_async_copy(arrived, arrived, bx_recv.at[slot, 0]).wait()
        weights, norm = weigh(direct[slot, 2, 0:count, :], direct[slot, 0])
        arrived = direct.at[slot, 1, pl.ds(count, (C - 1) * count), :]
        pltpu.make_async_copy(arrived, arrived, bx_recv.at[slot, 1]).wait()
        mixed = jnp.dot(weights, direct[slot, 1], preferred_element_type=jnp.float32)
        late[0, pl.ds(h - first, 1), :] = use(h, mixed / norm)

    @pl.loop(landed, heads - 1)
    def _(h):
        direct_head(h)

    if C > 1:
        others = part.at[pl.ds(1, C - 1)]
        pltpu.make_async_copy(others, others, p_recv).wait()
    acc = part[0]
    for r in range(1, C):
        acc = acc + part[r]
    total[0] = acc
    for r in range(1, D):
        pltpu.make_async_remote_copy(
            src_ref=total.at[0], dst_ref=total.at[r], send_sem=c_send, recv_sem=c_recv,
            device_id=clips[r - 1], device_id_type=MESH,
        ).start()
    pl.semaphore_wait(met_sem, C - 1)

    direct_head(heads - 1)
    order = sorted(range(1, n), key=lambda r: (r % D == 0) + (r < D or r > n - D))
    for r in order:
        pltpu.make_async_remote_copy(
            src_ref=late.at[0], dst_ref=late.at[r], send_sem=l_send, recv_sem=l_recv,
            device_id=peers[r - 1], device_id_type=MESH,
        ).start()

    gain_copy.wait_send()
    if D > 1:
        others = tbuf.at[pl.ds(1, D - 1)]
        pltpu.make_async_copy(others, others, t_send).wait()
        others = total.at[pl.ds(1, D - 1)]
        pltpu.make_async_copy(others, others, c_recv).wait()
        pltpu.make_async_copy(others, others, c_send).wait()
    if C > 1:
        others = part.at[pl.ds(1, C - 1)]
        pltpu.make_async_copy(others, others, p_send).wait()

    @pl.loop(0, first)
    def _(h):
        acc = emb[0] * total[0, pl.ds(h, 1), :]
        for j in range(1, D):
            acc = acc + emb[j] * total[j, pl.ds(h, 1), :]
        grad_ref[:, cols(h)] = acc

    @pl.loop(0, early)
    def _(h):
        sent = kv.at[h, :, pl.ds(count, (C - 1) * count), :]
        pltpu.make_async_copy(sent, sent, kv_send.at[h]).wait()
        pltpu.make_async_copy(abuf.at[h], abuf.at[h], a_send.at[h]).wait()

    @pl.loop(early, heads)
    def _(h):
        given = direct.at[heads - 1 - h, :, pl.ds(0, count), :]
        pltpu.make_async_copy(given, given, b_send.at[heads - 1 - h]).wait()

    @pl.loop(landed, heads)
    def _(h):
        for which in range(2):
            sent = direct.at[heads - 1 - h, which, pl.ds(count, (C - 1) * count), :]
            pltpu.make_async_copy(sent, sent, bx_send.at[heads - 1 - h, which]).wait()

    if n > 1:
        others = late.at[pl.ds(1, n - 1)]
        pltpu.make_async_copy(others, others, l_recv).wait()
        pltpu.make_async_copy(others, others, l_send).wait()

    sums = []
    for j in range(D):
        acc = late[j]
        for c in range(1, C):
            acc = acc + late[j + c * D]
        sums.append(acc)
    for i in range(tail):
        acc = emb[0] * sums[0][i : i + 1, :]
        for j in range(1, D):
            acc = acc + emb[j] * sums[j][i : i + 1, :]
        grad_ref[:, (first + i) * hd : (first + i + 1) * hd] = acc


def store(attn_ref, grad_ref, out_ref, grads_ref, out_sem, grad_sem):
    copies = [
        pltpu.make_async_copy(attn_ref, out_ref, out_sem),
        pltpu.make_async_copy(grad_ref, grads_ref, grad_sem),
    ]
    for copy in copies:
        copy.start()
    for copy in copies:
        copy.wait()


def local(S, C, D, qkv, qk_gain, mod_weight, positions, timesteps, cotangent):
    count, _, width = qkv.shape[2:]
    freqs = mod_weight.shape[1]
    heads = width // HEAD_DIM
    n = C * D
    rows = freqs // n
    hd = HEAD_DIM
    tail = min(TAIL, heads - 1)
    most = DIRECT + BONUS
    if S < 3 or n < 2 or tail < most or heads - most - LAG < 1:
        raise ValueError("unsupported mesh")
    bf, f32 = jnp.bfloat16, jnp.float32
    vmem = pl.BlockSpec(memory_space=pltpu.VMEM)
    hbm = pl.BlockSpec(memory_space=pltpu.HBM)
    dma = pltpu.SemaphoreType.DMA
    regular = pltpu.SemaphoreType.REGULAR
    pin = functools.partial(pltpu.with_memory_space_constraint, memory_space=pltpu.HBM)
    attn, grad = pl.pallas_call(
        functools.partial(body, S, C, D, heads, freqs),
        out_shape=(
            jax.ShapeDtypeStruct((count, width), bf),
            jax.ShapeDtypeStruct((rows, width), f32),
        ),
        in_specs=[hbm] * 4 + [pl.BlockSpec(memory_space=pltpu.SMEM), hbm],
        out_specs=(vmem, vmem),
        scratch_shapes=[
            pltpu.VMEM((2, count, width), bf),
            pltpu.VMEM((freqs, width), f32),
            pltpu.VMEM((count, width), bf),
            pltpu.VMEM((heads, 2, C * count, hd), bf),
            pltpu.VMEM((heads, count, hd), bf),
            pltpu.VMEM((heads, count, hd), bf),
            pltpu.VMEM((heads, count, hd), bf),
            pltpu.VMEM((most, 3, C * count, hd), bf),
            pltpu.VMEM((2, width), f32),
            pltpu.VMEM((1, count), jnp.int32),
            pltpu.VMEM((D, 8, hd), f32),
            pltpu.VMEM((-(-heads // 8) * 8, hd), f32),
            pltpu.VMEM((D, rows, hd), f32),
            pltpu.VMEM((count, hd), f32),
            pltpu.VMEM((count, hd), f32),
            pltpu.VMEM((C, heads - tail, hd), f32),
            pltpu.VMEM((D, heads - tail, hd), f32),
            pltpu.VMEM((n, tail, hd), f32),
            dma((5,)), dma((heads,)),
            dma((heads,)), dma((heads,)), dma((heads,)), dma((heads,)),
            dma, dma, dma, dma, dma, dma, dma, dma, dma, dma,
            dma((most,)), dma((most,)), dma((most, 2)), dma((most, 2)),
            regular, regular, regular, regular,
        ],
        compiler_params=pltpu.CompilerParams(
            collective_id=0, has_side_effects=True, vmem_limit_bytes=VMEM_LIMIT if C <= 2 else 60 << 20
        ),
    )(
        pin(jnp.moveaxis(qkv[0, 0], 1, 0)),
        pin(qk_gain[0]),
        pin(mod_weight[0]),
        pin(positions),
        timesteps,
        pin(cotangent[0, 0]),
    )
    anywhere = pl.BlockSpec(memory_space=pl.ANY)
    attn_out, gate_grad = pl.pallas_call(
        store,
        out_shape=(
            jax.ShapeDtypeStruct((count, width), bf),
            jax.ShapeDtypeStruct((rows, width), f32),
        ),
        in_specs=[anywhere, anywhere],
        out_specs=(anywhere, anywhere),
        scratch_shapes=[dma, dma],
        compiler_params=pltpu.CompilerParams(vmem_limit_bytes=4 << 20),
    )(attn, grad)
    return attn_out[None, None], gate_grad[None]


def solution(mesh):
    sizes = mesh.shape
    return jax.shard_map(
        functools.partial(local, sizes["segment"], sizes["ctx"], sizes["dp"]),
        mesh=mesh,
        in_specs=(
            P("segment", "dp", "ctx", None, None),
            P("segment", None, None),
            P("segment", None, None),
            P("dp", "ctx"),
            P("segment", "dp"),
            P("segment", "dp", "ctx", None),
        ),
        out_specs=(P("segment", "dp", "ctx", None), P("segment", ("ctx", "dp"), None)),
        check_vma=False,
    )
```

time: 49.3 us -> 48.4 us (0.982)
  Pallas kernels: 47.9 us -> 46.9 us
    pallas_call x1, Pallas kernels: 46.7 us -> 45.9 us  [local(): pl.pallas_call(functools.partial(body, S, C, D, heads, freqs), out_shape=...]
where the time goes in v1:
time: 48.4 us; the launch traced here: 48.2 us
  Pallas kernels  46.9 us (97%)
  between operations  1.29 us (3%)
    pallas_call x1, Pallas kernels, local(): pl.pallas_call(functools.partial(body, S, C, D, heads, freqs), out_shape=...  45.9 us
    pallas_call x1, Pallas kernels, local(): pl.pallas_call(store, out_shape=(jax.ShapeDtypeStruct((count, width), bf)...  1.01 us

profile of v1, /device:TPU:0, one launch (start us, length us, event | category | flops | bytes accessed | tf_op | source)
XLA Modules:
  0.0 48.2 jit_solution(10068926054578102709)
XLA Ops:
  1.3 45.9 %shard_map.77 = (bf16[160,2560]{1,0:T(8,128)(2,1)S(1)}, f32[32,2560]{1,0:T(8,128)S(1)}) custom-call(bf16[3,160,2560]{2,1,0:T(8,128)(2,1)} %bitcast.9, f32[2,2560]{1,0:T(2,128)} %bitcast.11, f32[256,2560]{1,0:T(8,128)} %bitcast.8, s32[1,160]{1,0:T(1,128)} %pos_ref.1, s32[1,1]{1,0:T(1,128)S(6)} %copy.8.t_ref, bf16[160,2560]{1,0:T(8,128)(2,1)} %bitcast.10), custom_call_target="tpu_custom_call" | custom-call | tf_op jit(solution)/shard_map/pallas_call | solution.py:473
  47.2 1.0 %shard_map.78 = (bf16[160,2560]{1,0:T(8,128)(2,1)}, f32[32,2560]{1,0:T(8,128)}) custom-call(bf16[160,2560]{1,0:T(8,128)(2,1)S(1)} %get-tuple-element.6.attn_ref, f32[32,2560]{1,0:T(8,128)S(1)} %get-tuple-element.7.grad_ref), custom_call_target="tpu_custom_call" | custom-call | tf_op jit(solution)/shard_map/pallas_call | solution.py:518

commit v2 on v1

--- a/solution.py
+++ b/solution.py
@@ -13,10 +13,10 @@
 GRID_COLS = 80
 MESH = pl.DeviceIdType.MESH
 LEAD = 12
-LAG = 6
+GROUP = 3
+LAG = 3
 DIRECT = 5
-BONUS = 0
-TAIL = 8
+FIRST = 9
 FORWARD_AT = 8
 VMEM_LIMIT = 24 << 20
 
@@ -57,34 +57,28 @@
     return jnp.where(group == 0, frame, jnp.where(group == 1, row, col)) * freq
 
 
-def handed(seg, S):
-    return DIRECT + jnp.where(seg == 0, BONUS, 0)
-
-
 def body(
     S, C, D, heads, freqs,
     x_ref, gain_ref, w_ref, pos_ref, t_ref, cot_ref,
     out_ref, grad_ref,
     xv, wv, cotv, kv, qbuf, abuf, rbuf, direct, gains, posv, tbuf, gate, emb, cosv, sinv,
-    part, total, late,
+    part, total, late, last,
     load_sem, v_sem, kv_send, kv_recv, a_send, a_recv, g_send, g_recv, t_send, t_recv,
-    p_send, p_recv, c_send, c_recv, l_send, l_recv,
-    b_send, b_recv, bx_send, bx_recv, in_sem, down_sem, up_sem, met_sem,
+    p_send, p_recv, c_send, c_recv, l_send, l_recv, m_send, m_recv,
+    b_send, b_recv, bx_send, bx_recv, in_sem, down_sem, up_sem, met_sem, dp_sem,
 ):
     n = C * D
     count = x_ref.shape[1]
     rows = freqs // n
     hd = HEAD_DIM
-    tail = late.shape[1]
-    first = heads - tail
+    first = part.shape[1]
     seg = lax.axis_index("segment")
     ctx = lax.axis_index("ctx")
     dp = lax.axis_index("dp")
     me = ctx * D + dp
     after = {"segment": lax.rem(seg + 1, S)}
     before = {"segment": lax.rem(seg + S - 1, S)}
-    early = heads - handed(seg, S)
-    landed = heads - handed(before["segment"], S)
+    early = heads - direct.shape[0]
     peers = []
     for r in range(1, n):
         p = lax.rem(me + r, n)
@@ -99,8 +93,12 @@
         pl.semaphore_signal(sem, inc=1, device_id=who, device_id_type=MESH)
 
     barrier = pltpu.get_barrier_semaphore()
-    for who in ring + clips:
+    for who in ring:
         tell(barrier, who)
+
+    @pl.loop(dp + 1, D)
+    def _(d):
+        tell(barrier, {"dp": d})
 
     @pl.when(seg < S - 1)
     def _():
@@ -113,17 +111,17 @@
         pltpu.make_async_copy(w_ref, wv, load_sem.at[3]),
         pltpu.make_async_copy(cot_ref, cotv, load_sem.at[4]),
     ]
-    for load in loads:
+    for load in loads[:3]:
         load.start()
 
-    pl.semaphore_wait(barrier, C - 1 + D - 1 + jnp.where(seg > 0, 1, 0))
+    pl.semaphore_wait(barrier, C - 1 + dp + jnp.where(seg > 0, 1, 0))
 
     def send_values(h):
         for r in range(1, C):
             pltpu.make_async_remote_copy(
                 src_ref=x_ref.at[2, :, cols(h)],
                 dst_ref=kv.at[h, 1, pl.ds(r * count, count), :],
-                send_sem=kv_send.at[h], recv_sem=kv_recv.at[h],
+                send_sem=kv_send, recv_sem=kv_recv.at[h],
                 device_id=ring[r - 1], device_id_type=MESH,
             ).start()
 
@@ -132,18 +130,26 @@
             pltpu.make_async_remote_copy(
                 src_ref=kv.at[h, 0, pl.ds(0, count), :],
                 dst_ref=kv.at[h, 0, pl.ds(r * count, count), :],
-                send_sem=kv_send.at[h], recv_sem=kv_recv.at[h],
+                send_sem=kv_send, recv_sem=kv_recv.at[h],
                 device_id=ring[r - 1], device_id_type=MESH,
             ).start()
 
-    lead = min(LEAD, heads - DIRECT - BONUS)
+    lead = min(LEAD, early)
 
     @pl.loop(0, lead)
     def _(h):
         send_values(h)
 
-    for who in ring:
-        tell(met_sem, who)
+    @pl.loop(0, dp)
+    def _(d):
+        tell(dp_sem, {"dp": d})
+
+    @pl.loop(0, heads)
+    def _(h):
+        pltpu.make_async_copy(x_ref.at[2, :, cols(h)], kv.at[h, 1, pl.ds(0, count), :], v_sem).start()
+
+    for load in loads[3:]:
+        load.start()
 
     gain_copy = pltpu.make_async_remote_copy(
         src_ref=gain_ref, dst_ref=gains, send_sem=g_send, recv_sem=g_recv,
@@ -187,25 +193,25 @@
         def _():
             tell(up_sem, after)
 
+    @pl.when(dp < D - 1)
+    def _():
+        pl.semaphore_wait(dp_sem, D - 1 - dp)
+
+    for who in ring:
+        tell(met_sem, who)
+    own = kv.at[:, 1, pl.ds(0, count), :]
+    pltpu.make_async_copy(own, own, v_sem).wait()
+
     def hand_over(source, which, h):
         slot = heads - 1 - h
         pltpu.make_async_remote_copy(
             src_ref=source, dst_ref=direct.at[slot, which, pl.ds(0, count), :],
-            send_sem=b_send.at[slot], recv_sem=b_recv.at[slot], device_id=after, device_id_type=MESH,
+            send_sem=b_send, recv_sem=b_recv, device_id=after, device_id_type=MESH,
         ).start()
 
-    def own_values(h):
-        return pltpu.make_async_copy(
-            x_ref.at[2, :, cols(h)], kv.at[h, 1, pl.ds(0, count), :], v_sem.at[h]
-        )
-
     @pl.loop(early, heads)
     def _(h):
-        hand_over(x_ref.at[2, :, cols(h)], 1, h)
-
-    @pl.loop(0, early)
-    def _(h):
-        own_values(h).start()
+        hand_over(kv.at[h, 1, pl.ds(0, count), :], 1, h)
 
     loads[0].wait()
     pos = jnp.transpose(jnp.broadcast_to(posv[...], (hd, count)))
@@ -242,16 +248,23 @@
     gain_copy.wait_recv()
 
     def forward(slot):
-        here = direct.at[slot, :, pl.ds(0, count), :]
-        pltpu.make_async_copy(here, here, b_recv.at[slot]).wait()
         for which in range(2):
             for r in range(1, C):
                 pltpu.make_async_remote_copy(
                     src_ref=direct.at[slot, which, pl.ds(0, count), :],
                     dst_ref=direct.at[slot, which, pl.ds(r * count, count), :],
-                    send_sem=bx_send.at[slot, which], recv_sem=bx_recv.at[slot, which],
+                    send_sem=bx_send, recv_sem=bx_recv.at[slot * 2 + which],
                     device_id=ring[r - 1], device_id_type=MESH,
                 ).start()
+
+    @pl.loop(0, early)
+    def _(h):
+        kv[h, 0, 0:count, :] = turned(1, h, inv_k)
+        send_keys(h)
+
+        @pl.when(h + lead < early)
+        def _():
+            send_values(h + lead)
 
     @pl.loop(early, heads)
     def _(h):
@@ -259,15 +272,6 @@
         qbuf[h] = turned(0, h, inv_q)
         hand_over(kv.at[h, 0, pl.ds(0, count), :], 0, h)
         hand_over(qbuf.at[h], 2, h)
-
-    @pl.loop(0, early)
-    def _(h):
-        kv[h, 0, 0:count, :] = turned(1, h, inv_k)
-        send_keys(h)
-
-        @pl.when(h + lead < early)
-        def _():
-            send_values(h + lead)
 
     @pl.loop(0, early)
     def _(h):
@@ -304,14 +308,13 @@
         return expo.astype(jnp.bfloat16), jnp.sum(expo, axis=1, keepdims=True)
 
     def attend(h):
-        own_values(h).wait()
         arrived = kv.at[h, :, pl.ds(count, (C - 1) * count), :]
         pltpu.make_async_copy(arrived, arrived, kv_recv.at[h]).wait()
         weights, norm = weigh(qbuf[h], kv[h, 0])
         mixed = jnp.dot(weights, kv[h, 1], preferred_element_type=jnp.float32)
         abuf[h] = (mixed / norm).astype(jnp.bfloat16)
         pltpu.make_async_remote_copy(
-            src_ref=abuf.at[h], dst_ref=rbuf.at[h], send_sem=a_send.at[h], recv_sem=a_recv.at[h],
+            src_ref=abuf.at[h], dst_ref=rbuf.at[h], send_sem=a_send, recv_sem=a_recv.at[h // GROUP],
             device_id=after, device_id_type=MESH,
         ).start()
 
@@ -320,9 +323,12 @@
         cot = cotv[:, cols(h)].astype(jnp.float32)
         return jnp.sum(attn * cot, axis=0, keepdims=True)
 
-    def finish(h):
-        pltpu.make_async_copy(rbuf.at[h], rbuf.at[h], a_recv.at[h]).wait()
-        return use(h, rbuf[h].astype(jnp.float32))
+    def finish(g):
+        some = rbuf.at[pl.ds(g * GROUP, GROUP)]
+        pltpu.make_async_copy(some, some, a_recv.at[g]).wait()
+        for i in range(GROUP):
+            h = g * GROUP + i
+            part[0, pl.ds(h, 1), :] = use(h, rbuf[h].astype(jnp.float32))
 
     @pl.loop(0, early)
     def _(h):
@@ -330,42 +336,66 @@
 
         @pl.when(h == FORWARD_AT)
         def _():
-            @pl.loop(landed, heads - 1)
+            here = direct.at[:, :, pl.ds(0, count), :]
+            pltpu.make_async_copy(here, here, b_recv).wait()
+
+            @pl.loop(early, heads - 1)
             def _(g):
                 forward(heads - 1 - g)
 
-        @pl.when(h >= LAG)
+        @pl.when(jnp.logical_and(lax.rem(h, GROUP) == GROUP - 1, h >= LAG * GROUP))
         def _():
-            part[0, pl.ds(h - LAG, 1), :] = finish(h - LAG)
-
-    @pl.loop(early - LAG, first)
-    def _(h):
-        part[0, pl.ds(h, 1), :] = finish(h)
+            finish(h // GROUP - LAG)
+
+    groups = early // GROUP
+
+    @pl.loop(max(groups - LAG, 0), first // GROUP)
+    def _(g):
+        finish(g)
 
     for r in range(1, C):
         pltpu.make_async_remote_copy(
             src_ref=part.at[0], dst_ref=part.at[r], send_sem=p_send, recv_sem=p_recv,
             device_id=ring[r - 1], device_id_type=MESH,
         ).start()
-    forward(0)
-
-    @pl.loop(first, landed)
-    def _(h):
-        late[0, pl.ds(h - first, 1), :] = finish(h)
 
     def direct_head(h):
         slot = heads - 1 - h
-        arrived = direct.at[slot, 0, pl.ds(count, (C - 1) * count), :]
-        pltpu.make_async_copy(arrived, arrived, bx_recv.at[slot, 0]).wait()
-        weights, norm = weigh(direct[slot, 2, 0:count, :], direct[slot, 0])
-        arrived = direct.at[slot, 1, pl.ds(count, (C - 1) * count), :]
-        pltpu.make_async_copy(arrived, arrived, bx_recv.at[slot, 1]).wait()
+        for which in range(2):
+            arrived = direct.at[slot, which, pl.ds(count, (C - 1) * count), :]
+            pltpu.make_async_copy(arrived, arrived, bx_recv.at[slot * 2 + which]).wait()
+            if which == 0:
+                weights, norm = weigh(direct[slot, 2, 0:count, :], direct[slot, 0])
         mixed = jnp.dot(weights, direct[slot, 1], preferred_element_type=jnp.float32)
-        late[0, pl.ds(h - first, 1), :] = use(h, mixed / norm)
-
-    @pl.loop(landed, heads - 1)
-    def _(h):
-        direct_head(h)
+        return use(h, mixed / norm)
+
+    forward(0)
+
+    @pl.loop(early, heads - 1)
+    def _(h):
+        late[0, pl.ds(h - first, 1), :] = direct_head(h)
+
+    @pl.loop(first // GROUP, groups)
+    def _(g):
+        some = rbuf.at[pl.ds(g * GROUP, GROUP)]
+        pltpu.make_async_copy(some, some, a_recv.at[g]).wait()
+        for i in range(GROUP):
+            h = g * GROUP + i
+            late[0, pl.ds(h - first, 1), :] = use(h, rbuf[h].astype(jnp.float32))
+
+    pl.semaphore_wait(met_sem, C - 1)
+    order = sorted(range(1, n), key=lambda r: (r % D == 0) + (r < D or r > n - D))
+
+    def share(rows_of, send, recv):
+        for r in order:
+            pltpu.make_async_remote_copy(
+                src_ref=rows_of.at[0], dst_ref=rows_of.at[r], send_sem=send, recv_sem=recv,
+                device_id=peers[r - 1], device_id_type=MESH,
+            ).start()
+
+    share(late, l_send, l_recv)
+    last[0] = direct_head(heads - 1)
+    share(last, m_send, m_recv)
 
     if C > 1:
         others = part.at[pl.ds(1, C - 1)]
@@ -379,15 +409,6 @@
             src_ref=total.at[0], dst_ref=total.at[r], send_sem=c_send, recv_sem=c_recv,
             device_id=clips[r - 1], device_id_type=MESH,
         ).start()
-    pl.semaphore_wait(met_sem, C - 1)
-
-    direct_head(heads - 1)
-    order = sorted(range(1, n), key=lambda r: (r % D == 0) + (r < D or r > n - D))
-    for r in order:
-        pltpu.make_async_remote_copy(
-            src_ref=late.at[0], dst_ref=late.at[r], send_sem=l_send, recv_sem=l_recv,
-            device_id=peers[r - 1], device_id_type=MESH,
-        ).start()
 
     gain_copy.wait_send()
     if D > 1:
@@ -407,39 +428,33 @@
             acc = acc + emb[j] * total[j, pl.ds(h, 1), :]
         grad_ref[:, cols(h)] = acc
 
-    @pl.loop(0, early)
-    def _(h):
-        sent = kv.at[h, :, pl.ds(count, (C - 1) * count), :]
-        pltpu.make_async_copy(sent, sent, kv_send.at[h]).wait()
-        pltpu.make_async_copy(abuf.at[h], abuf.at[h], a_send.at[h]).wait()
-
-    @pl.loop(early, heads)
-    def _(h):
-        given = direct.at[heads - 1 - h, :, pl.ds(0, count), :]
-        pltpu.make_async_copy(given, given, b_send.at[heads - 1 - h]).wait()
-
-    @pl.loop(landed, heads)
-    def _(h):
-        for which in range(2):
-            sent = direct.at[heads - 1 - h, which, pl.ds(count, (C - 1) * count), :]
-            pltpu.make_async_copy(sent, sent, bx_send.at[heads - 1 - h, which]).wait()
-
-    if n > 1:
-        others = late.at[pl.ds(1, n - 1)]
-        pltpu.make_async_copy(others, others, l_recv).wait()
-        pltpu.make_async_copy(others, others, l_send).wait()
-
-    sums = []
-    for j in range(D):
-        acc = late[j]
-        for c in range(1, C):
-            acc = acc + late[j + c * D]
-        sums.append(acc)
-    for i in range(tail):
-        acc = emb[0] * sums[0][i : i + 1, :]
-        for j in range(1, D):
-            acc = acc + emb[j] * sums[j][i : i + 1, :]
-        grad_ref[:, (first + i) * hd : (first + i + 1) * hd] = acc
+    sent = kv.at[pl.ds(0, early), :, pl.ds(count, (C - 1) * count), :]
+    pltpu.make_async_copy(sent, sent, kv_send).wait()
+    sent = abuf.at[pl.ds(0, early)]
+    pltpu.make_async_copy(sent, sent, a_send).wait()
+    sent = direct.at[:, :, pl.ds(0, count), :]
+    pltpu.make_async_copy(sent, sent, b_send).wait()
+    sent = direct.at[:, pl.ds(0, 2), pl.ds(count, (C - 1) * count), :]
+    pltpu.make_async_copy(sent, sent, bx_send).wait()
+
+    def grads(rows_of, recv, send, start):
+        others = rows_of.at[pl.ds(1, n - 1)]
+        pltpu.make_async_copy(others, others, recv).wait()
+        sums = []
+        for j in range(D):
+            acc = rows_of[j]
+            for c in range(1, C):
+                acc = acc + rows_of[j + c * D]
+            sums.append(acc)
+        for i in range(rows_of.shape[1]):
+            acc = emb[0] * sums[0][i : i + 1, :]
+            for j in range(1, D):
+                acc = acc + emb[j] * sums[j][i : i + 1, :]
+            grad_ref[:, (start + i) * hd : (start + i + 1) * hd] = acc
+        pltpu.make_async_copy(others, others, send).wait()
+
+    grads(late, l_recv, l_send, first)
+    grads(last, m_recv, m_send, heads - 1)
 
 
 def store(attn_ref, grad_ref, out_ref, grads_ref, out_sem, grad_sem):
@@ -460,9 +475,10 @@
     n = C * D
     rows = freqs // n
     hd = HEAD_DIM
-    tail = min(TAIL, heads - 1)
-    most = DIRECT + BONUS
-    if S < 3 or n < 2 or tail < most or heads - most - LAG < 1:
+    most = DIRECT
+    early = heads - most
+    first = FIRST
+    if S < 3 or n < 2 or early % GROUP or first % GROUP or first > early or FORWARD_AT >= early:
         raise ValueError("unsupported mesh")
     bf, f32 = jnp.bfloat16, jnp.float32
     vmem = pl.BlockSpec(memory_space=pltpu.VMEM)
@@ -494,14 +510,15 @@
             pltpu.VMEM((D, rows, hd), f32),
             pltpu.VMEM((count, hd), f32),
             pltpu.VMEM((count, hd), f32),
-            pltpu.VMEM((C, heads - tail, hd), f32),
-            pltpu.VMEM((D, heads - tail, hd), f32),
-            pltpu.VMEM((n, tail, hd), f32),
-            dma((5,)), dma((heads,)),
-            dma((heads,)), dma((heads,)), dma((heads,)), dma((heads,)),
-            dma, dma, dma, dma, dma, dma, dma, dma, dma, dma,
-            dma((most,)), dma((most,)), dma((most, 2)), dma((most, 2)),
-            regular, regular, regular, regular,
+            pltpu.VMEM((C, first, hd), f32),
+            pltpu.VMEM((D, first, hd), f32),
+            pltpu.VMEM((n, heads - 1 - first, hd), f32),
+            pltpu.VMEM((n, 1, hd), f32),
+            dma((5,)), dma,
+            dma, dma((early,)), dma, dma((early // GROUP,)),
+            dma, dma, dma, dma, dma, dma, dma, dma, dma, dma, dma, dma,
+            dma, dma, dma, dma((most * 2,)),
+            regular, regular, regular, regular, regular,
         ],
         compiler_params=pltpu.CompilerParams(
             collective_id=0, has_side_effects=True, vmem_limit_bytes=VMEM_LIMIT if C <= 2 else 60 << 20

time: 48.4 us -> 46.7 us (0.965)
  Pallas kernels: 46.9 us -> 45.2 us
    pallas_call x1, Pallas kernels: 45.9 us -> 44.2 us  [local(): pl.pallas_call(functools.partial(body, S, C, D, heads, freqs), out_shape=...]
where the time goes in v2:
time: 46.7 us; the launch traced here: 46.5 us
  Pallas kernels  45.2 us (97%)
  between operations  1.29 us (3%)
    pallas_call x1, Pallas kernels, local(): pl.pallas_call(functools.partial(body, S, C, D, heads, freqs), out_shape=...  44.2 us
    pallas_call x1, Pallas kernels, local(): pl.pallas_call(store, out_shape=(jax.ShapeDtypeStruct((count, width), bf)...  1.01 us

profile of v2, /device:TPU:0, one launch (start us, length us, event | category | flops | bytes accessed | tf_op | source)
XLA Modules:
  0.0 46.5 jit_solution(870921140086548014)
XLA Ops:
  1.3 44.2 %shard_map.77 = (bf16[160,2560]{1,0:T(8,128)(2,1)S(1)}, f32[32,2560]{1,0:T(8,128)S(1)}) custom-call(bf16[3,160,2560]{2,1,0:T(8,128)(2,1)} %bitcast.9, f32[2,2560]{1,0:T(2,128)} %bitcast.11, f32[256,2560]{1,0:T(8,128)} %bitcast.8, s32[1,160]{1,0:T(1,128)} %pos_ref.1, s32[1,1]{1,0:T(1,128)S(6)} %copy.8.t_ref, bf16[160,2560]{1,0:T(8,128)(2,1)} %bitcast.10), custom_call_target="tpu_custom_call" | custom-call | tf_op jit(solution)/shard_map/pallas_call | solution.py:489
  45.5 1.0 %shard_map.78 = (bf16[160,2560]{1,0:T(8,128)(2,1)}, f32[32,2560]{1,0:T(8,128)}) custom-call(bf16[160,2560]{1,0:T(8,128)(2,1)S(1)} %get-tuple-element.6.attn_ref, f32[32,2560]{1,0:T(8,128)S(1)} %get-tuple-element.7.grad_ref), custom_call_target="tpu_custom_call" | custom-call | tf_op jit(solution)/shard_map/pallas_call | solution.py:535

commit v3 on v2

--- a/solution.py
+++ b/solution.py
@@ -17,6 +17,7 @@
 LAG = 3
 DIRECT = 5
 FIRST = 9
+GIVER = 0
 FORWARD_AT = 8
 VMEM_LIMIT = 24 << 20
 
@@ -65,7 +66,7 @@
     part, total, late, last,
     load_sem, v_sem, kv_send, kv_recv, a_send, a_recv, g_send, g_recv, t_send, t_recv,
     p_send, p_recv, c_send, c_recv, l_send, l_recv, m_send, m_recv,
-    b_send, b_recv, bx_send, bx_recv, in_sem, down_sem, up_sem, met_sem, dp_sem,
+    b_send, b_recv, bx_send, bx_recv, e_send, e_recv, ex_send, ex_recv, in_sem, down_sem, up_sem, met_sem, dp_sem,
 ):
     n = C * D
     count = x_ref.shape[1]
@@ -78,7 +79,12 @@
     me = ctx * D + dp
     after = {"segment": lax.rem(seg + 1, S)}
     before = {"segment": lax.rem(seg + S - 1, S)}
-    early = heads - direct.shape[0]
+    most = direct.shape[0] - 1
+    early = heads - most
+    edge = dp == D - 1
+    give = jnp.logical_and(seg == GIVER, edge)
+    take = jnp.logical_and(seg == GIVER + 1, edge)
+    mine = early - jnp.where(give, 1, 0)
     peers = []
     for r in range(1, n):
         p = lax.rem(me + r, n)
@@ -111,8 +117,6 @@
         pltpu.make_async_copy(w_ref, wv, load_sem.at[3]),
         pltpu.make_async_copy(cot_ref, cotv, load_sem.at[4]),
     ]
-    for load in loads[:3]:
-        load.start()
 
     pl.semaphore_wait(barrier, C - 1 + dp + jnp.where(seg > 0, 1, 0))
 
@@ -134,7 +138,7 @@
                 device_id=ring[r - 1], device_id_type=MESH,
             ).start()
 
-    lead = min(LEAD, early)
+    lead = min(LEAD, early - 1)
 
     @pl.loop(0, lead)
     def _(h):
@@ -144,12 +148,13 @@
     def _(d):
         tell(dp_sem, {"dp": d})
 
+    for load in loads[:3]:
+        load.start()
+
     @pl.loop(0, heads)
     def _(h):
         pltpu.make_async_copy(x_ref.at[2, :, cols(h)], kv.at[h, 1, pl.ds(0, count), :], v_sem).start()
 
-    for load in loads[3:]:
-        load.start()
 
     gain_copy = pltpu.make_async_remote_copy(
         src_ref=gain_ref, dst_ref=gains, send_sem=g_send, recv_sem=g_recv,
@@ -202,11 +207,13 @@
     own = kv.at[:, 1, pl.ds(0, count), :]
     pltpu.make_async_copy(own, own, v_sem).wait()
 
-    def hand_over(source, which, h):
-        slot = heads - 1 - h
+    for load in loads[3:]:
+        load.start()
+
+    def hand_over(source, which, h, send=b_send, recv=b_recv):
         pltpu.make_async_remote_copy(
-            src_ref=source, dst_ref=direct.at[slot, which, pl.ds(0, count), :],
-            send_sem=b_send, recv_sem=b_recv, device_id=after, device_id_type=MESH,
+            src_ref=source, dst_ref=direct.at[heads - 1 - h, which, pl.ds(0, count), :],
+            send_sem=send, recv_sem=recv, device_id=after, device_id_type=MESH,
         ).start()
 
     @pl.loop(early, heads)
@@ -247,22 +254,22 @@
     inv_q = inverse_norm(0)
     gain_copy.wait_recv()
 
-    def forward(slot):
+    def forward(slot, sems, send=bx_send):
         for which in range(2):
             for r in range(1, C):
                 pltpu.make_async_remote_copy(
                     src_ref=direct.at[slot, which, pl.ds(0, count), :],
                     dst_ref=direct.at[slot, which, pl.ds(r * count, count), :],
-                    send_sem=bx_send, recv_sem=bx_recv.at[slot * 2 + which],
+                    send_sem=send, recv_sem=sems[which],
                     device_id=ring[r - 1], device_id_type=MESH,
                 ).start()
 
-    @pl.loop(0, early)
+    @pl.loop(0, mine)
     def _(h):
         kv[h, 0, 0:count, :] = turned(1, h, inv_k)
         send_keys(h)
 
-        @pl.when(h + lead < early)
+        @pl.when(h + lead < mine)
         def _():
             send_values(h + lead)
 
@@ -273,7 +280,17 @@
         hand_over(kv.at[h, 0, pl.ds(0, count), :], 0, h)
         hand_over(qbuf.at[h], 2, h)
 
-    @pl.loop(0, early)
+    spare = early - 1
+
+    @pl.when(give)
+    def _():
+        kv[spare, 0, 0:count, :] = turned(1, spare, inv_k)
+        qbuf[spare] = turned(0, spare, inv_q)
+        hand_over(kv.at[spare, 1, pl.ds(0, count), :], 1, spare, e_send, e_recv)
+        hand_over(kv.at[spare, 0, pl.ds(0, count), :], 0, spare, e_send, e_recv)
+        hand_over(qbuf.at[spare], 2, spare, e_send, e_recv)
+
+    @pl.loop(0, mine)
     def _(h):
         qbuf[h] = turned(0, h, inv_q)
 
@@ -330,18 +347,25 @@
             h = g * GROUP + i
             part[0, pl.ds(h, 1), :] = use(h, rbuf[h].astype(jnp.float32))
 
-    @pl.loop(0, early)
+    @pl.loop(0, mine)
     def _(h):
         attend(h)
 
         @pl.when(h == FORWARD_AT)
         def _():
-            here = direct.at[:, :, pl.ds(0, count), :]
+            here = direct.at[pl.ds(0, most), :, pl.ds(0, count), :]
             pltpu.make_async_copy(here, here, b_recv).wait()
+
+            @pl.when(take)
+            def _():
+                more = direct.at[most, :, pl.ds(0, count), :]
+                pltpu.make_async_copy(more, more, e_recv).wait()
+                forward(most, (ex_recv, ex_recv), ex_send)
 
             @pl.loop(early, heads - 1)
             def _(g):
-                forward(heads - 1 - g)
+                slot = heads - 1 - g
+                forward(slot, (bx_recv.at[slot - 1], bx_recv.at[slot - 1]))
 
         @pl.when(jnp.logical_and(lax.rem(h, GROUP) == GROUP - 1, h >= LAG * GROUP))
         def _():
@@ -349,7 +373,7 @@
 
     groups = early // GROUP
 
-    @pl.loop(max(groups - LAG, 0), first // GROUP)
+    @pl.loop(mine // GROUP - LAG, first // GROUP)
     def _(g):
         finish(g)
 
@@ -359,29 +383,42 @@
             device_id=ring[r - 1], device_id_type=MESH,
         ).start()
 
-    def direct_head(h):
+    forward(0, (bx_recv.at[most - 1], bx_recv.at[most]))
+
+    def direct_head(h, sem):
         slot = heads - 1 - h
-        for which in range(2):
-            arrived = direct.at[slot, which, pl.ds(count, (C - 1) * count), :]
-            pltpu.make_async_copy(arrived, arrived, bx_recv.at[slot * 2 + which]).wait()
-            if which == 0:
-                weights, norm = weigh(direct[slot, 2, 0:count, :], direct[slot, 0])
+        arrived = direct.at[slot, pl.ds(0, 2), pl.ds(count, (C - 1) * count), :]
+        pltpu.make_async_copy(arrived, arrived, sem).wait()
+        weights, norm = weigh(direct[slot, 2, 0:count, :], direct[slot, 0])
         mixed = jnp.dot(weights, direct[slot, 1], preferred_element_type=jnp.float32)
-        return use(h, mixed / norm)
-
-    forward(0)
+        late[0, pl.ds(h - first, 1), :] = use(h, mixed / norm)
+
+    @pl.when(take)
+    def _():
+        direct_head(spare, ex_recv)
 
     @pl.loop(early, heads - 1)
     def _(h):
-        late[0, pl.ds(h - first, 1), :] = direct_head(h)
-
-    @pl.loop(first // GROUP, groups)
-    def _(g):
-        some = rbuf.at[pl.ds(g * GROUP, GROUP)]
+        direct_head(h, bx_recv.at[heads - 2 - h])
+
+    def results(g, size):
+        some = rbuf.at[pl.ds(g * GROUP, size)]
         pltpu.make_async_copy(some, some, a_recv.at[g]).wait()
-        for i in range(GROUP):
+        for i in range(size):
             h = g * GROUP + i
             late[0, pl.ds(h - first, 1), :] = use(h, rbuf[h].astype(jnp.float32))
+
+    @pl.loop(first // GROUP, groups - 1)
+    def _(g):
+        results(g, GROUP)
+
+    @pl.when(take)
+    def _():
+        results(groups - 1, GROUP - 1)
+
+    @pl.when(jnp.logical_not(take))
+    def _():
+        results(groups - 1, GROUP)
 
     pl.semaphore_wait(met_sem, C - 1)
     order = sorted(range(1, n), key=lambda r: (r % D == 0) + (r < D or r > n - D))
@@ -394,9 +431,6 @@
             ).start()
 
     share(late, l_send, l_recv)
-    last[0] = direct_head(heads - 1)
-    share(last, m_send, m_recv)
-
     if C > 1:
         others = part.at[pl.ds(1, C - 1)]
         pltpu.make_async_copy(others, others, p_recv).wait()
@@ -410,6 +444,20 @@
             device_id=clips[r - 1], device_id_type=MESH,
         ).start()
 
+    final = slice((heads - 1) * hd, heads * hd)
+    arrived = direct.at[0, 0, pl.ds(count, (C - 1) * count), :]
+    pltpu.make_async_copy(arrived, arrived, bx_recv.at[most - 1]).wait()
+    weights, norm = weigh(direct[0, 2, 0:count, :], direct[0, 0])
+    inverse = 1.0 / norm
+    cot = cotv[:, final].astype(jnp.float32) * inverse
+    arrived = direct.at[0, 1, pl.ds(count, (C - 1) * count), :]
+    pltpu.make_async_copy(arrived, arrived, bx_recv.at[most]).wait()
+    mixed = jnp.dot(weights, direct[0, 1], preferred_element_type=jnp.float32)
+    last[0] = jnp.sum(mixed * cot, axis=0, keepdims=True)
+    share(last, m_send, m_recv)
+    out_ref[:, final] = (mixed * inverse * gate[heads - 1 : heads, :]).astype(jnp.bfloat16)
+
+
     gain_copy.wait_send()
     if D > 1:
         others = tbuf.at[pl.ds(1, D - 1)]
@@ -428,13 +476,30 @@
             acc = acc + emb[j] * total[j, pl.ds(h, 1), :]
         grad_ref[:, cols(h)] = acc
 
-    sent = kv.at[pl.ds(0, early), :, pl.ds(count, (C - 1) * count), :]
-    pltpu.make_async_copy(sent, sent, kv_send).wait()
-    sent = abuf.at[pl.ds(0, early)]
-    pltpu.make_async_copy(sent, sent, a_send).wait()
-    sent = direct.at[:, :, pl.ds(0, count), :]
+    def drain(number):
+        sent = kv.at[pl.ds(0, number), :, pl.ds(count, (C - 1) * count), :]
+        pltpu.make_async_copy(sent, sent, kv_send).wait()
+        sent = abuf.at[pl.ds(0, number)]
+        pltpu.make_async_copy(sent, sent, a_send).wait()
+
+    @pl.when(give)
+    def _():
+        drain(early - 1)
+        sent = direct.at[most, :, pl.ds(0, count), :]
+        pltpu.make_async_copy(sent, sent, e_send).wait()
+
+    @pl.when(jnp.logical_not(give))
+    def _():
+        drain(early)
+
+    @pl.when(take)
+    def _():
+        sent = direct.at[most, pl.ds(0, 2), pl.ds(count, (C - 1) * count), :]
+        pltpu.make_async_copy(sent, sent, ex_send).wait()
+
+    sent = direct.at[pl.ds(0, most), :, pl.ds(0, count), :]
     pltpu.make_async_copy(sent, sent, b_send).wait()
-    sent = direct.at[:, pl.ds(0, 2), pl.ds(count, (C - 1) * count), :]
+    sent = direct.at[pl.ds(0, most), pl.ds(0, 2), pl.ds(count, (C - 1) * count), :]
     pltpu.make_async_copy(sent, sent, bx_send).wait()
 
     def grads(rows_of, recv, send, start):
@@ -478,7 +543,7 @@
     most = DIRECT
     early = heads - most
     first = FIRST
-    if S < 3 or n < 2 or early % GROUP or first % GROUP or first > early or FORWARD_AT >= early:
+    if S < 3 or n < 2 or early % GROUP or first % GROUP or first + GROUP > early or FORWARD_AT >= early:
         raise ValueError("unsupported mesh")
     bf, f32 = jnp.bfloat16, jnp.float32
     vmem = pl.BlockSpec(memory_space=pltpu.VMEM)
@@ -502,7 +567,7 @@
             pltpu.VMEM((heads, count, hd), bf),
             pltpu.VMEM((heads, count, hd), bf),
             pltpu.VMEM((heads, count, hd), bf),
-            pltpu.VMEM((most, 3, C * count, hd), bf),
+            pltpu.VMEM((most + 1, 3, C * count, hd), bf),
             pltpu.VMEM((2, width), f32),
             pltpu.VMEM((1, count), jnp.int32),
             pltpu.VMEM((D, 8, hd), f32),
@@ -517,7 +582,7 @@
             dma((5,)), dma,
             dma, dma((early,)), dma, dma((early // GROUP,)),
             dma, dma, dma, dma, dma, dma, dma, dma, dma, dma, dma, dma,
-            dma, dma, dma, dma((most * 2,)),
+            dma, dma, dma, dma((most + 1,)), dma, dma, dma, dma,
             regular, regular, regular, regular, regular,
         ],
         compiler_params=pltpu.CompilerParams(

time: 46.7 us -> 46 us (0.985)
  Pallas kernels: 45.2 us -> 44.5 us
    pallas_call x1, Pallas kernels: 44.2 us -> 43.5 us  [local(): pl.pallas_call(functools.partial(body, S, C, D, heads, freqs), out_shape=...]
where the time goes in v3:
time: 46 us; the launch traced here: 45.8 us
  Pallas kernels  44.5 us (97%)
  between operations  1.29 us (3%)
    pallas_call x1, Pallas kernels, local(): pl.pallas_call(functools.partial(body, S, C, D, heads, freqs), out_shape=...  43.5 us
    pallas_call x1, Pallas kernels, local(): pl.pallas_call(store, out_shape=(jax.ShapeDtypeStruct((count, width), bf)...  1.01 us

profile of v3, /device:TPU:0, one launch (start us, length us, event | category | flops | bytes accessed | tf_op | source)
XLA Modules:
  0.0 45.8 jit_solution(13822958046393977828)
XLA Ops:
  1.3 43.5 %shard_map.77 = (bf16[160,2560]{1,0:T(8,128)(2,1)S(1)}, f32[32,2560]{1,0:T(8,128)S(1)}) custom-call(bf16[3,160,2560]{2,1,0:T(8,128)(2,1)} %bitcast.9, f32[2,2560]{1,0:T(2,128)} %bitcast.11, f32[256,2560]{1,0:T(8,128)} %bitcast.8, s32[1,160]{1,0:T(1,128)} %pos_ref.1, s32[1,1]{1,0:T(1,128)S(6)} %copy.8.t_ref, bf16[160,2560]{1,0:T(8,128)(2,1)} %bitcast.10), custom_call_target="tpu_custom_call" | custom-call | tf_op jit(solution)/shard_map/pallas_call | solution.py:554
  44.8 1.0 %shard_map.78 = (bf16[160,2560]{1,0:T(8,128)(2,1)}, f32[32,2560]{1,0:T(8,128)}) custom-call(bf16[160,2560]{1,0:T(8,128)(2,1)S(1)} %get-tuple-element.6.attn_ref, f32[32,2560]{1,0:T(8,128)S(1)} %get-tuple-element.7.grad_ref), custom_call_target="tpu_custom_call" | custom-call | tf_op jit(solution)/shard_map/pallas_call | solution.py:600

commit v4 on v3

--- a/solution.py
+++ b/solution.py
@@ -63,10 +63,10 @@
     x_ref, gain_ref, w_ref, pos_ref, t_ref, cot_ref,
     out_ref, grad_ref,
     xv, wv, cotv, kv, qbuf, abuf, rbuf, direct, gains, posv, tbuf, gate, emb, cosv, sinv,
-    part, total, late, last,
+    part, total, late, last, ubuf, ures,
     load_sem, v_sem, kv_send, kv_recv, a_send, a_recv, g_send, g_recv, t_send, t_recv,
     p_send, p_recv, c_send, c_recv, l_send, l_recv, m_send, m_recv,
-    b_send, b_recv, bx_send, bx_recv, e_send, e_recv, ex_send, ex_recv, in_sem, down_sem, up_sem, met_sem, dp_sem,
+    b_send, b_recv, bx_send, bx_recv, e_send, e_recv, ex_send, ex_recv, u_send, u_recv, ur_send, in_sem, down_sem, up_sem, met_sem, dp_sem,
 ):
     n = C * D
     count = x_ref.shape[1]
@@ -85,6 +85,10 @@
     give = jnp.logical_and(seg == GIVER, edge)
     take = jnp.logical_and(seg == GIVER + 1, edge)
     mine = early - jnp.where(give, 1, 0)
+    swap = jnp.logical_and(dp == D - 2, C == 2)
+    host = jnp.logical_and(swap, ctx == 0)
+    guest = jnp.logical_and(swap, ctx == 1)
+    low = jnp.where(swap, 1, 0)
     peers = []
     for r in range(1, n):
         p = lax.rem(me + r, n)
@@ -102,9 +106,23 @@
     for who in ring:
         tell(barrier, who)
 
-    @pl.loop(dp + 1, D)
-    def _(d):
-        tell(barrier, {"dp": d})
+    pairs = D == 4
+    if pairs:
+        @pl.when(dp < 2)
+        def _():
+            tell(barrier, {"dp": dp + 2})
+
+        @pl.when(lax.rem(dp, 2) == 1)
+        def _():
+            tell(barrier, {"dp": dp - 1})
+
+        met = jnp.where(dp >= 2, 1, 0) + jnp.where(lax.rem(dp, 2) == 0, 1, 0)
+    else:
+        @pl.loop(dp + 1, D)
+        def _(d):
+            tell(barrier, {"dp": d})
+
+        met = dp
 
     @pl.when(seg < S - 1)
     def _():
@@ -118,7 +136,7 @@
         pltpu.make_async_copy(cot_ref, cotv, load_sem.at[4]),
     ]
 
-    pl.semaphore_wait(barrier, C - 1 + dp + jnp.where(seg > 0, 1, 0))
+    pl.semaphore_wait(barrier, C - 1 + met + jnp.where(seg > 0, 1, 0))
 
     def send_values(h):
         for r in range(1, C):
@@ -138,15 +156,21 @@
                 device_id=ring[r - 1], device_id_type=MESH,
             ).start()
 
-    lead = min(LEAD, early - 1)
-
-    @pl.loop(0, lead)
+    lead = min(LEAD, early - 2)
+
+    @pl.loop(low, low + lead)
     def _(h):
         send_values(h)
 
-    @pl.loop(0, dp)
-    def _(d):
-        tell(dp_sem, {"dp": d})
+    if pairs:
+        @pl.when(dp == 2)
+        def _():
+            tell(dp_sem, {"dp": dp - 2})
+            tell(dp_sem, {"dp": dp + 1})
+    else:
+        @pl.loop(0, dp)
+        def _(d):
+            tell(dp_sem, {"dp": d})
 
     for load in loads[:3]:
         load.start()
@@ -198,9 +222,17 @@
         def _():
             tell(up_sem, after)
 
-    @pl.when(dp < D - 1)
-    def _():
-        pl.semaphore_wait(dp_sem, D - 1 - dp)
+    if pairs:
+        pl.semaphore_wait(dp_sem, 1)
+
+        @pl.when(dp == 0)
+        def _():
+            tell(dp_sem, {"dp": dp + 1})
+            tell(dp_sem, {"dp": dp + 2})
+    else:
+        @pl.when(dp < D - 1)
+        def _():
+            pl.semaphore_wait(dp_sem, D - 1 - dp)
 
     for who in ring:
         tell(met_sem, who)
@@ -264,7 +296,20 @@
                     device_id=ring[r - 1], device_id_type=MESH,
                 ).start()
 
-    @pl.loop(0, mine)
+    @pl.when(swap)
+    def _():
+        kv[0, 0, 0:count, :] = turned(1, 0, inv_k)
+        qbuf[0] = turned(0, 0, inv_q)
+
+    @pl.when(guest)
+    def _():
+        for i, source in enumerate((kv.at[0, 0, pl.ds(0, count), :], kv.at[0, 1, pl.ds(0, count), :], qbuf.at[0])):
+            pltpu.make_async_remote_copy(
+                src_ref=source, dst_ref=ubuf.at[i], send_sem=u_send, recv_sem=u_recv,
+                device_id=ring[0], device_id_type=MESH,
+            ).start()
+
+    @pl.loop(low, mine)
     def _(h):
         kv[h, 0, 0:count, :] = turned(1, h, inv_k)
         send_keys(h)
@@ -290,7 +335,7 @@
         hand_over(kv.at[spare, 0, pl.ds(0, count), :], 0, spare, e_send, e_recv)
         hand_over(qbuf.at[spare], 2, spare, e_send, e_recv)
 
-    @pl.loop(0, mine)
+    @pl.loop(low, mine)
     def _(h):
         qbuf[h] = turned(0, h, inv_q)
 
@@ -347,7 +392,25 @@
             h = g * GROUP + i
             part[0, pl.ds(h, 1), :] = use(h, rbuf[h].astype(jnp.float32))
 
-    @pl.loop(0, mine)
+    @pl.when(host)
+    def _():
+        some = ubuf.at[pl.ds(0, 3)]
+        pltpu.make_async_copy(some, some, u_recv).wait()
+        kv[0, 0, count : 2 * count, :] = ubuf[0]
+        kv[0, 1, count : 2 * count, :] = ubuf[1]
+        ubuf[3] = qbuf[0]
+
+        @pl.loop(0, 2)
+        def _(i):
+            weights, norm = weigh(ubuf[2 + i], kv[0, 0])
+            mixed = jnp.dot(weights, kv[0, 1], preferred_element_type=jnp.float32)
+            ures[i] = (mixed / norm).astype(jnp.bfloat16)
+            pltpu.make_async_remote_copy(
+                src_ref=ures.at[i], dst_ref=rbuf.at[0], send_sem=ur_send, recv_sem=a_recv.at[0],
+                device_id={"segment": after["segment"], "ctx": 1 - i}, device_id_type=MESH,
+            ).start()
+
+    @pl.loop(low, mine)
     def _(h):
         attend(h)
 
@@ -482,15 +545,29 @@
         sent = abuf.at[pl.ds(0, number)]
         pltpu.make_async_copy(sent, sent, a_send).wait()
 
+    fewer = jnp.logical_or(give, swap)
+
+    @pl.when(fewer)
+    def _():
+        drain(early - 1)
+
+    @pl.when(jnp.logical_not(fewer))
+    def _():
+        drain(early)
+
     @pl.when(give)
     def _():
-        drain(early - 1)
         sent = direct.at[most, :, pl.ds(0, count), :]
         pltpu.make_async_copy(sent, sent, e_send).wait()
 
-    @pl.when(jnp.logical_not(give))
-    def _():
-        drain(early)
+    @pl.when(guest)
+    def _():
+        sent = ubuf.at[pl.ds(0, 3)]
+        pltpu.make_async_copy(sent, sent, u_send).wait()
+
+    @pl.when(host)
+    def _():
+        pltpu.make_async_copy(ures, ures, ur_send).wait()
 
     @pl.when(take)
     def _():
@@ -543,7 +620,7 @@
     most = DIRECT
     early = heads - most
     first = FIRST
-    if S < 3 or n < 2 or early % GROUP or first % GROUP or first + GROUP > early or FORWARD_AT >= early:
+    if S < 3 or C < 2 or D < 2 or early % GROUP or first % GROUP or first + GROUP > early or FORWARD_AT >= early:
         raise ValueError("unsupported mesh")
     bf, f32 = jnp.bfloat16, jnp.float32
     vmem = pl.BlockSpec(memory_space=pltpu.VMEM)
@@ -579,10 +656,12 @@
             pltpu.VMEM((D, first, hd), f32),
             pltpu.VMEM((n, heads - 1 - first, hd), f32),
             pltpu.VMEM((n, 1, hd), f32),
+            pltpu.VMEM((4, count, hd), bf),
+            pltpu.VMEM((2, count, hd), bf),
             dma((5,)), dma,
             dma, dma((early,)), dma, dma((early // GROUP,)),
             dma, dma, dma, dma, dma, dma, dma, dma, dma, dma, dma, dma,
-            dma, dma, dma, dma((most + 1,)), dma, dma, dma, dma,
+            dma, dma, dma, dma((most + 1,)), dma, dma, dma, dma, dma, dma, dma,
             regular, regular, regular, regular, regular,
         ],
         compiler_params=pltpu.CompilerParams(

time: 46 us -> 45.9 us (level)
  no operation moved by 1% of the time
where the time goes in v4:
time: 45.9 us; the launch traced here: 45.7 us
  Pallas kernels  44.4 us (97%)
  between operations  1.29 us (3%)
    pallas_call x1, Pallas kernels, local(): pl.pallas_call(functools.partial(body, S, C, D, heads, freqs), out_shape=...  43.4 us
    pallas_call x1, Pallas kernels, local(): pl.pallas_call(store, out_shape=(jax.ShapeDtypeStruct((count, width), bf)...  1.01 us

profile of v4, /device:TPU:0, one launch (start us, length us, event | category | flops | bytes accessed | tf_op | source)
XLA Modules:
  0.0 45.7 jit_solution(4773760756194682931)
XLA Ops:
  1.3 43.4 %shard_map.77 = (bf16[160,2560]{1,0:T(8,128)(2,1)S(1)}, f32[32,2560]{1,0:T(8,128)S(1)}) custom-call(bf16[3,160,2560]{2,1,0:T(8,128)(2,1)} %bitcast.9, f32[2,2560]{1,0:T(2,128)} %bitcast.11, f32[256,2560]{1,0:T(8,128)} %bitcast.8, s32[1,160]{1,0:T(1,128)} %pos_ref.1, s32[1,1]{1,0:T(1,128)S(6)} %copy.8.t_ref, bf16[160,2560]{1,0:T(8,128)(2,1)} %bitcast.10), custom_call_target="tpu_custom_call" | custom-call | tf_op jit(solution)/shard_map/pallas_call | solution.py:631
  44.7 1.0 %shard_map.78 = (bf16[160,2560]{1,0:T(8,128)(2,1)}, f32[32,2560]{1,0:T(8,128)}) custom-call(bf16[160,2560]{1,0:T(8,128)(2,1)S(1)} %get-tuple-element.6.attn_ref, f32[32,2560]{1,0:T(8,128)S(1)} %get-tuple-element.7.grad_ref), custom_call_target="tpu_custom_call" | custom-call | tf_op jit(solution)/shard_map/pallas_call | solution.py:679

commit v5 on v4

--- a/solution.py
+++ b/solution.py
@@ -16,8 +16,8 @@
 GROUP = 3
 LAG = 3
 DIRECT = 5
-FIRST = 9
-GIVER = 0
+FIRST = 6
+FAR = 2
 FORWARD_AT = 8
 VMEM_LIMIT = 24 << 20
 
@@ -81,9 +81,12 @@
     before = {"segment": lax.rem(seg + S - 1, S)}
     most = direct.shape[0] - 1
     early = heads - most
-    edge = dp == D - 1
-    give = jnp.logical_and(seg == GIVER, edge)
-    take = jnp.logical_and(seg == GIVER + 1, edge)
+    def gives(at):
+        reach = jnp.where(dp == D - 1, 1, jnp.where(dp == D - 3, FAR, 0))
+        return at < reach
+
+    give = gives(seg)
+    take = jnp.logical_and(seg > 0, gives(seg - 1))
     mine = early - jnp.where(give, 1, 0)
     swap = jnp.logical_and(dp == D - 2, C == 2)
     host = jnp.logical_and(swap, ctx == 0)
@@ -460,40 +463,10 @@
     def _():
         direct_head(spare, ex_recv)
 
-    @pl.loop(early, heads - 1)
+    @pl.loop(early, heads - 2)
     def _(h):
         direct_head(h, bx_recv.at[heads - 2 - h])
 
-    def results(g, size):
-        some = rbuf.at[pl.ds(g * GROUP, size)]
-        pltpu.make_async_copy(some, some, a_recv.at[g]).wait()
-        for i in range(size):
-            h = g * GROUP + i
-            late[0, pl.ds(h - first, 1), :] = use(h, rbuf[h].astype(jnp.float32))
-
-    @pl.loop(first // GROUP, groups - 1)
-    def _(g):
-        results(g, GROUP)
-
-    @pl.when(take)
-    def _():
-        results(groups - 1, GROUP - 1)
-
-    @pl.when(jnp.logical_not(take))
-    def _():
-        results(groups - 1, GROUP)
-
-    pl.semaphore_wait(met_sem, C - 1)
-    order = sorted(range(1, n), key=lambda r: (r % D == 0) + (r < D or r > n - D))
-
-    def share(rows_of, send, recv):
-        for r in order:
-            pltpu.make_async_remote_copy(
-                src_ref=rows_of.at[0], dst_ref=rows_of.at[r], send_sem=send, recv_sem=recv,
-                device_id=peers[r - 1], device_id_type=MESH,
-            ).start()
-
-    share(late, l_send, l_recv)
     if C > 1:
         others = part.at[pl.ds(1, C - 1)]
         pltpu.make_async_copy(others, others, p_recv).wait()
@@ -507,6 +480,38 @@
             device_id=clips[r - 1], device_id_type=MESH,
         ).start()
 
+    direct_head(heads - 2, bx_recv.at[0])
+
+    def results(g, size):
+        some = rbuf.at[pl.ds(g * GROUP, size)]
+        pltpu.make_async_copy(some, some, a_recv.at[g]).wait()
+        for i in range(size):
+            h = g * GROUP + i
+            late[0, pl.ds(h - first, 1), :] = use(h, rbuf[h].astype(jnp.float32))
+
+    @pl.loop(first // GROUP, groups - 1)
+    def _(g):
+        results(g, GROUP)
+
+    @pl.when(take)
+    def _():
+        results(groups - 1, GROUP - 1)
+
+    @pl.when(jnp.logical_not(take))
+    def _():
+        results(groups - 1, GROUP)
+
+    pl.semaphore_wait(met_sem, C - 1)
+    order = sorted(range(1, n), key=lambda r: (r % D == 0) + (r < D or r > n - D))
+
+    def share(rows_of, send, recv):
+        for r in order:
+            pltpu.make_async_remote_copy(
+                src_ref=rows_of.at[0], dst_ref=rows_of.at[r], send_sem=send, recv_sem=recv,
+                device_id=peers[r - 1], device_id_type=MESH,
+            ).start()
+
+    share(late, l_send, l_recv)
     final = slice((heads - 1) * hd, heads * hd)
     arrived = direct.at[0, 0, pl.ds(count, (C - 1) * count), :]
     pltpu.make_async_copy(arrived, arrived, bx_recv.at[most - 1]).wait()

time: 45.9 us -> 45.7 us (level)
  no operation moved by 1% of the time
where the time goes in v5:
time: 45.7 us; the launch traced here: 45.5 us
  Pallas kernels  44.2 us (97%)
  between operations  1.29 us (3%)
    pallas_call x1, Pallas kernels, local(): pl.pallas_call(functools.partial(body, S, C, D, heads, freqs), out_shape=...  43.2 us
    pallas_call x1, Pallas kernels, local(): pl.pallas_call(store, out_shape=(jax.ShapeDtypeStruct((count, width), bf)...  1.01 us

profile of v5, /device:TPU:0, one launch (start us, length us, event | category | flops | bytes accessed | tf_op | source)
XLA Modules:
  0.0 45.5 jit_solution(4769788002529170300)
XLA Ops:
  1.3 43.2 %shard_map.77 = (bf16[160,2560]{1,0:T(8,128)(2,1)S(1)}, f32[32,2560]{1,0:T(8,128)S(1)}) custom-call(bf16[3,160,2560]{2,1,0:T(8,128)(2,1)} %bitcast.9, f32[2,2560]{1,0:T(2,128)} %bitcast.11, f32[256,2560]{1,0:T(8,128)} %bitcast.8, s32[1,160]{1,0:T(1,128)} %pos_ref.1, s32[1,1]{1,0:T(1,128)S(6)} %copy.8.t_ref, bf16[160,2560]{1,0:T(8,128)(2,1)} %bitcast.10), custom_call_target="tpu_custom_call" | custom-call | tf_op jit(solution)/shard_map/pallas_call | solution.py:636
  44.5 1.0 %shard_map.78 = (bf16[160,2560]{1,0:T(8,128)(2,1)}, f32[32,2560]{1,0:T(8,128)}) custom-call(bf16[160,2560]{1,0:T(8,128)(2,1)S(1)} %get-tuple-element.6.attn_ref, f32[32,2560]{1,0:T(8,128)S(1)} %get-tuple-element.7.grad_ref), custom_call_target="tpu_custom_call" | custom-call | tf_op jit(solution)/shard_map/pallas_call | solution.py:684

commit v6 on v5

--- a/solution.py
+++ b/solution.py
@@ -13,11 +13,12 @@
 GRID_COLS = 80
 MESH = pl.DeviceIdType.MESH
 LEAD = 12
-GROUP = 3
-LAG = 3
+GROUP = 5
+LAG = 2
 DIRECT = 5
-FIRST = 6
+FIRST = 5
 FAR = 2
+PAIRED = 10
 FORWARD_AT = 8
 VMEM_LIMIT = 24 << 20
 
@@ -141,12 +142,17 @@
 
     pl.semaphore_wait(barrier, C - 1 + met + jnp.where(seg > 0, 1, 0))
 
+    solo = PAIRED + 1
+
+    def spot(h):
+        return jnp.minimum(h + 1, PAIRED + 2) // 2 + jnp.maximum(h - solo, 0)
+
     def send_values(h):
         for r in range(1, C):
             pltpu.make_async_remote_copy(
                 src_ref=x_ref.at[2, :, cols(h)],
                 dst_ref=kv.at[h, 1, pl.ds(r * count, count), :],
-                send_sem=kv_send, recv_sem=kv_recv.at[h],
+                send_sem=kv_send, recv_sem=kv_recv.at[spot(h)],
                 device_id=ring[r - 1], device_id_type=MESH,
             ).start()
 
@@ -155,7 +161,7 @@
             pltpu.make_async_remote_copy(
                 src_ref=kv.at[h, 0, pl.ds(0, count), :],
                 dst_ref=kv.at[h, 0, pl.ds(r * count, count), :],
-                send_sem=kv_send, recv_sem=kv_recv.at[h],
+                send_sem=kv_send, recv_sem=kv_recv.at[spot(h)],
                 device_id=ring[r - 1], device_id_type=MESH,
             ).start()
 
@@ -373,8 +379,16 @@
         return expo.astype(jnp.bfloat16), jnp.sum(expo, axis=1, keepdims=True)
 
     def attend(h):
-        arrived = kv.at[h, :, pl.ds(count, (C - 1) * count), :]
-        pltpu.make_async_copy(arrived, arrived, kv_recv.at[h]).wait()
+        @pl.when(jnp.logical_and(lax.rem(h, 2) == 1, h < solo))
+        def _():
+            arrived = kv.at[pl.ds(h, 2), :, pl.ds(count, (C - 1) * count), :]
+            pltpu.make_async_copy(arrived, arrived, kv_recv.at[spot(h)]).wait()
+
+        @pl.when(jnp.logical_or(h == 0, h >= solo))
+        def _():
+            arrived = kv.at[h, :, pl.ds(count, (C - 1) * count), :]
+            pltpu.make_async_copy(arrived, arrived, kv_recv.at[spot(h)]).wait()
+
         weights, norm = weigh(qbuf[h], kv[h, 0])
         mixed = jnp.dot(weights, kv[h, 1], preferred_element_type=jnp.float32)
         abuf[h] = (mixed / norm).astype(jnp.bfloat16)
@@ -625,7 +639,7 @@
     most = DIRECT
     early = heads - most
     first = FIRST
-    if S < 3 or C < 2 or D < 2 or early % GROUP or first % GROUP or first + GROUP > early or FORWARD_AT >= early:
+    if S < 3 or C < 2 or D < 2 or early % GROUP or first % GROUP or first + GROUP > early or PAIRED + 2 > early or FORWARD_AT >= early:
         raise ValueError("unsupported mesh")
     bf, f32 = jnp.bfloat16, jnp.float32
     vmem = pl.BlockSpec(memory_space=pltpu.VMEM)
@@ -664,7 +678,7 @@
             pltpu.VMEM((4, count, hd), bf),
             pltpu.VMEM((2, count, hd), bf),
             dma((5,)), dma,
-            dma, dma((early,)), dma, dma((early // GROUP,)),
+            dma, dma((early - PAIRED // 2,)), dma, dma((early // GROUP,)),
             dma, dma, dma, dma, dma, dma, dma, dma, dma, dma, dma, dma,
             dma, dma, dma, dma((most + 1,)), dma, dma, dma, dma, dma, dma, dma,
             regular, regular, regular, regular, regular,

time: 45.7 us -> 45.5 us (level)
  no operation moved by 1% of the time
where the time goes in v6:
time: 45.5 us; the launch traced here: 45.4 us
  Pallas kernels  44.1 us (97%)
  between operations  1.29 us (3%)
    pallas_call x1, Pallas kernels, local(): pl.pallas_call(functools.partial(body, S, C, D, heads, freqs), out_shape=...  43.1 us
    pallas_call x1, Pallas kernels, local(): pl.pallas_call(store, out_shape=(jax.ShapeDtypeStruct((count, width), bf)...  1.01 us

profile of v6, /device:TPU:0, one launch (start us, length us, event | category | flops | bytes accessed | tf_op | source)
XLA Modules:
  0.0 45.4 jit_solution(237307589886021543)
XLA Ops:
  1.3 43.1 %shard_map.77 = (bf16[160,2560]{1,0:T(8,128)(2,1)S(1)}, f32[32,2560]{1,0:T(8,128)S(1)}) custom-call(bf16[3,160,2560]{2,1,0:T(8,128)(2,1)} %bitcast.9, f32[2,2560]{1,0:T(2,128)} %bitcast.11, f32[256,2560]{1,0:T(8,128)} %bitcast.8, s32[1,160]{1,0:T(1,128)} %pos_ref.1, s32[1,1]{1,0:T(1,128)S(6)} %copy.8.t_ref, bf16[160,2560]{1,0:T(8,128)(2,1)} %bitcast.10), custom_call_target="tpu_custom_call" | custom-call | tf_op jit(solution)/shard_map/pallas_call | solution.py:650
  44.3 1.0 %shard_map.78 = (bf16[160,2560]{1,0:T(8,128)(2,1)}, f32[32,2560]{1,0:T(8,128)}) custom-call(bf16[160,2560]{1,0:T(8,128)(2,1)S(1)} %get-tuple-element.6.attn_ref, f32[32,2560]{1,0:T(8,128)S(1)} %get-tuple-element.7.grad_ref), custom_call_target="tpu_custom_call" | custom-call | tf_op jit(solution)/shard_map/pallas_call | solution.py:698
